TPU v7x, 32 devices: a whole 2x2x4 slice. The times are simulated.
32 devices in a mesh: patch: 2 (over x), sim: 16 (over z, y, core).
Axes of the slice: x: 2, y: 2, z: 4, core: 2. Of those that a mesh axis runs over, the one named last changes fastest.
Arguments:
- sky_maps: bfloat16 [2048, 2048], P(('patch', 'sim')), parts along dimension 0, may hold values from -6 to 6
- ivf_maps: bfloat16 [2048, 2048], P(('patch', 'sim')), parts along dimension 0, may hold values from -6 to 6
- sim_sky: bfloat16 [8, 2048, 2048], P(None, ('patch', 'sim')), parts along dimension 1, may hold values from -6 to 6
- sim_ivf: bfloat16 [8, 2048, 2048], P(None, ('patch', 'sim')), parts along dimension 1, may hold values from -6 to 6
- ra_wiener: bfloat16 [1024, 1024], replicated, may hold values from -0.1875 to 0.1875
- ra_gradient: bfloat16 [1024, 1024], replicated, may hold values from -0.1875 to 0.1875
- pair_table: int32 [8, 8], replicated, may hold values 0 or 1
- sim_index: int32 [4], replicated, may hold values from 0 to 7
- source_pixels: int32 [8192], P('patch'), parts along dimension 0, may hold values from 0 to 262143
- response: float32 [256], P('patch'), parts along dimension 0, may hold values from 0.2 to 2
Outputs:
- lens_split: float32 [2048, 2048], P(('patch', 'sim')), parts along dimension 0
There are 2 independent parts, one for each index of `patch`. A program takes and returns all parts, laid end to end along the dimension named above; an argument that names none is the same for every part. Nothing has to cross between parts.
Inputs may be any that keep to these rules, and one draw needn't show every extreme that they name: `sim_index`: indices into the cached evolutions; entries may repeat. `source_pixels`: flat pixel indices of the patch; entries may repeat.
All inputs are finite; a program needn't handle non-finite values.
Results may differ from a plain program's by a relative error of at most 0.0035.
Values may be sent and summed in bfloat16 or wider, within the bound.
A program may use at most 128 MiB of HBM per device.

v0:
```python
import jax
import jax.numpy as jnp
from jax import lax
from jax.sharding import PartitionSpec as P

NSPLIT = 8
NUSE = 4


def extended(cells, sides, width):
    for axis, dim in sides:
        count = lax.axis_size(axis)
        head = lax.slice_in_dim(cells, 0, width, axis=dim)
        tail = lax.slice_in_dim(cells, cells.shape[dim] - width, cells.shape[dim], axis=dim)
        cells = jnp.concatenate(
            [
                lax.ppermute(tail, axis, [(i, (i + 1) % count) for i in range(count)]),
                cells,
                lax.ppermute(head, axis, [((i + 1) % count, i) for i in range(count)]),
            ],
            axis=dim,
        )
    return cells


def from_behind(block, axis, distance):
    devices = range(lax.axis_size(axis))
    route = [((i - distance) % len(devices), i) for i in devices]
    return lax.ppermute(block, axis, route)


def tile_apply(values, matrix):
    width = matrix.shape[0]
    shaped = values.reshape(values.shape[:-1] + (values.shape[-1] // width, width))
    result = jnp.einsum("...tc,cd->...td", shaped, matrix, preferred_element_type=jnp.float32)
    return result.reshape(values.shape)


def trim_edges(padded, band_index, group_bands):
    lower_keep = (band_index > 0).astype(padded.dtype)
    upper_keep = (band_index < group_bands - 1).astype(padded.dtype)
    return jnp.concatenate(
        [padded[:, :1] * lower_keep, padded[:, 1:-1], padded[:, -1:] * upper_keep], axis=1
    )


def row_slope(padded):
    upper = padded[:, 2:].astype(jnp.float32)
    lower = padded[:, :-2].astype(jnp.float32)
    return (upper - lower) * 0.5


def on_device(
    sky_maps,
    ivf_maps,
    sim_sky,
    sim_ivf,
    ra_wiener,
    ra_gradient,
    pair_table,
    sim_index,
    source_pixels,
    response,
):
    axis_count = lax.axis_size("sim")
    group_bands = axis_count // NSPLIT
    device_index = lax.axis_index("sim")
    logical = (device_index - group_bands // 2) % axis_count
    band_index = logical % group_bands
    split_index = logical // group_bands
    rows = sky_maps.shape[0]
    columns = sky_maps.shape[1]
    chosen_sky = jnp.concatenate([sky_maps[None], jnp.take(sim_sky, sim_index, axis=0)], axis=0)
    chosen_ivf = jnp.concatenate([ivf_maps[None], jnp.take(sim_ivf, sim_index, axis=0)], axis=0)
    offsets = source_pixels - band_index * rows * columns
    inside = (offsets >= 0) & (offsets < rows * columns)
    offsets = jnp.where(inside, offsets, rows * columns)
    hit = jnp.zeros((rows * columns,), jnp.bfloat16).at[offsets].set(1, mode="drop")
    keep = (1 - hit).reshape(rows, columns)
    masked = chosen_ivf * keep[None]
    wiener = tile_apply(chosen_sky, ra_wiener).astype(jnp.bfloat16)
    padded = extended(masked, (("sim", 1),), 1)
    padded = trim_edges(padded, band_index, group_bands)
    pair_row = lax.dynamic_index_in_dim(pair_table, split_index, 0, keepdims=False)
    others = jnp.arange(NSPLIT) != split_index
    weights_row = jnp.where(others, pair_row, 0).astype(jnp.float32)
    empty = jnp.zeros(masked.shape, jnp.float32)
    totals = (empty, empty, empty)
    moving = padded
    for step in range(NSPLIT - 1):
        moving = from_behind(moving, "sim", group_bands)
        factor = weights_row[(split_index - step - 1) % NSPLIT]
        middle = moving[:, 1:-1]
        absorb_total_ra = totals[0] + factor * tile_apply(middle, ra_gradient)
        absorb_total_dec = totals[1] + factor * row_slope(moving)
        absorb_total_src = totals[2] + factor * middle.astype(jnp.float32)
        totals = (absorb_total_ra, absorb_total_dec, absorb_total_src)
    total_ra, total_dec, total_src = totals
    wiener_wide = wiener.astype(jnp.float32)
    flux_ra = (wiener_wide * total_ra).astype(jnp.bfloat16)
    flux_dec = wiener_wide * total_dec
    flux_pad = extended(flux_dec.astype(jnp.bfloat16), (("sim", 1),), 1).astype(flux_dec.dtype)
    flux_pad = trim_edges(flux_pad, band_index, group_bands)
    divergence = tile_apply(flux_ra, ra_gradient) + row_slope(flux_pad)
    weight_rows = lax.dynamic_slice_in_dim(response, band_index * rows, rows)
    hardened = -divergence - weight_rows[None, :, None] * (wiener_wide * total_src)
    return hardened[0] - jnp.sum(hardened[1:], axis=0) / NUSE


def solution(mesh):
    in_specs = (
        P(("patch", "sim"), None),
        P(("patch", "sim"), None),
        P(None, ("patch", "sim"), None),
        P(None, ("patch", "sim"), None),
        P(),
        P(),
        P(),
        P(),
        P("patch"),
        P("patch"),
    )
    out_specs = P(("patch", "sim"), None)
    return jax.shard_map(
        on_device, mesh=mesh, in_specs=in_specs, out_specs=out_specs, check_vma=False
    )
```

profile of v0, /device:TPU:1, one launch (start us, length us, event | category | flops | bytes accessed | tf_op | source)
XLA Modules:
  0.0 324.7 jit_solution(11645422656141791755)
XLA Ops:
  0.0 0.8 compare_select_fusion.1
  0.8 0.7 compare_and_fusion
  1.5 2.2 gather_fusion.1
  3.7 3.2 gather_fusion
  6.9 28.7 %scatter_custom_fusion = bf16[131072]{0:T(1024)(128)(2,1)S(1)} fusion(s32[4096]{0:T(1024)S(1)} %compare_select_fusion, bf16[4096]{0:T(1024)(128)(2,1)S(1)} %broadcast.54, bf16[]{:T(256)} %constant.125.clone.1), kind=kCustom, calls=%fused_computation.60 | custom fusion | bytes 262146 | tf_op jit(solution)/shard_map/scatter | solution.py:78
  35.6 0.7 broadcast_subtract_fusion
  36.3 1.8 mul.218
  38.1 2.5 broadcast_select_fusion
  40.6 0.1 maximum_multiply_fusion
  40.9 2.7 collective-permute-start
  43.6 1.7 collective-permute-done.1
  45.3 0.8 broadcast_multiply_fusion
  46.2 1.0 collective-permute-done
  47.2 0.4 pad_maximum_fusion.2
  47.6 1.2 collective-permute-start.2
  48.8 33.6 %collective-permute-done.2 = bf16[5,66,2048]{2,1,0:T(8,128)(2,1)S(1)} collective-permute-done((bf16[5,66,2048]{2,1,0:T(8,128)(2,1)S(1)}, bf16[5,66,2048]{2,1,0:T(8,128)(2,1)S(1)}, u32[]{:S(2)}, u32[]{:S(2)}) %collective-permute-start.2) | collective-permute-done | bytes 1351712 | tf_op jit(solution)/shard_map/ppermute | solution.py:29
  82.4 1.1 copy-done.3
  83.6 32.1 %collective-permute-done.3 = bf16[5,66,2048]{2,1,0:T(8,128)(2,1)S(1)} collective-permute-done((bf16[5,66,2048]{2,1,0:T(8,128)(2,1)S(1)}, bf16[5,66,2048]{2,1,0:T(8,128)(2,1)S(1)}, u32[]{:S(2)}, u32[]{:S(2)}) %collective-permute-start.3) | collective-permute-done | bytes 1351712 | tf_op jit(solution)/shard_map/ppermute | solution.py:29
  115.6 1.1 copy-done.6
  116.8 31.2 %collective-permute-done.4 = bf16[5,66,2048]{2,1,0:T(8,128)(2,1)S(1)} collective-permute-done((bf16[5,66,2048]{2,1,0:T(8,128)(2,1)S(1)}, bf16[5,66,2048]{2,1,0:T(8,128)(2,1)S(1)}, u32[]{:S(2)}, u32[]{:S(2)}) %collective-permute-start.4) | collective-permute-done | bytes 1351712 | tf_op jit(solution)/shard_map/ppermute | solution.py:29
  148.0 1.2 copy-done.9
  149.2 32.0 %collective-permute-done.5 = bf16[5,66,2048]{2,1,0:T(8,128)(2,1)} collective-permute-done((bf16[5,66,2048]{2,1,0:T(8,128)(2,1)S(1)}, bf16[5,66,2048]{2,1,0:T(8,128)(2,1)}, u32[]{:S(2)}, u32[]{:S(2)}) %collective-permute-start.5) | collective-permute-done | bytes 1351712 | tf_op jit(solution)/shard_map/ppermute | solution.py:29
  181.2 0.1 collective-permute-start.6
  181.3 1.1 copy.65
  182.4 1.1 concatenate.24
  183.6 28.6 %collective-permute-done.6 = bf16[5,66,2048]{2,1,0:T(8,128)(2,1)} collective-permute-done((bf16[5,66,2048]{2,1,0:T(8,128)(2,1)}, bf16[5,66,2048]{2,1,0:T(8,128)(2,1)}, u32[]{:S(2)}, u32[]{:S(2)}) %collective-permute-start.6) | collective-permute-done | bytes 1351712 | tf_op jit(solution)/shard_map/ppermute | solution.py:29
  212.2 0.6 collective-permute-start.7
  212.8 3.4 %fusion.29 = bf16[5,64,2,1024]{3,1,2,0:T(8,128)(2,1)S(1)} fusion(bf16[1024,1024]{1,0:T(8,128)(2,1)} %param.16, bf16[4,64,2,1024]{3,1,2,0:T(8,128)(2,1)} %bitcast.97, bf16[1,64,2,1024]{3,1,2,0:T(8,128)(2,1)S(1)} %copy.11), kind=kOutput, calls=%fused_computation.34 | convolution fusion | flops 1343488000 | bytes 4718592 | tf_op jit(solution)/shard_map/...tc,cd->...td/dot_general | solution.py:35
  216.5 0.3 convert_bitcast_fusion
  216.8 1.7 copy.33
  218.5 0.7 fusion.56
  219.2 0.7 fusion.60
  224.4 1.7 slice.136
  226.1 3.1 fusion.22
  229.2 0.3 slice.137
  229.6 3.0 fusion.20
  232.6 0.3 slice.138
  232.9 10.1 %collective-permute-done.7 = bf16[5,66,2048]{2,1,0:T(8,128)(2,1)} collective-permute-done((bf16[5,66,2048]{2,1,0:T(8,128)(2,1)}, bf16[5,66,2048]{2,1,0:T(8,128)(2,1)}, u32[]{:S(2)}, u32[]{:S(2)}) %collective-permute-start.7) | collective-permute-done | bytes 1351712 | tf_op jit(solution)/shard_map/ppermute | solution.py:29
  243.0 0.6 collective-permute-start.8
  243.6 3.1 fusion.18
  246.7 1.7 slice.139
  248.4 3.1 fusion.16
  251.6 1.7 slice.140
  253.3 3.1 fusion.14
  256.3 1.7 slice.141
  258.0 3.1 fusion.12
  261.1 12.5 %collective-permute-done.8 = bf16[5,66,2048]{2,1,0:T(8,128)(2,1)S(1)} collective-permute-done((bf16[5,66,2048]{2,1,0:T(8,128)(2,1)}, bf16[5,66,2048]{2,1,0:T(8,128)(2,1)S(1)}, u32[]{:S(2)}, u32[]{:S(2)}) %collective-permute-start.8) | collective-permute-done | bytes 1351712 | tf_op jit(solution)/shard_map/ppermute | solution.py:29
  273.6 7.0 %multiply_convert_fusion = bf16[5,64,2048]{2,1,0:T(8,128)(2,1)S(1)} fusion(f32[5,64,2048]{2,1,0:T(8,128)S(1)} %bitcast.86, bf16[5,66,2048]{2,1,0:T(8,128)(2,1)S(1)} %collective-permute-done.8, bf16[5,66,2048]{2,1,0:T(8,128)(2,1)} %collective-permute-done.7, bf16[5,66,2048]{2,1,0:T(8,128)(2,1)} %collective-permute-done.6, ...), kind=kLoop, calls=%fused_computation.13 | loop fusion | flops 23592960 | bytes 22282268 | tf_op jit(solution)/shard_map/convert_element_type | solution.py:102
  280.7 0.7 fusion.58
  281.3 8.6 %collective-permute-start.10 = (bf16[5,1,2048]{2,1,0:T(2,128)(2,1)}, bf16[5,1,2048]{2,1,0:T(2,128)(2,1)S(1)}, u32[]{:S(2)}, u32[]{:S(2)}) collective-permute-start(bf16[5,1,2048]{2,1,0:T(2,128)(2,1)} %get-tuple-element.9), channel_id=1, source_target_pairs={{1,0},{2,1},{3,2},{4,3},{5,4},{6,5},{7,6},{8,7},{9,8},{10,9},{11,1... | collective-permute-start | bytes 61448 | tf_op jit(solution)/shard_map/ppermute | solution.py:19
  289.9 1.4 slice.142
  291.4 15.8 %fusion.26 = f32[5,2,8,8,1024]{4,3,2,1,0:T(8,128)} fusion(bf16[1024,1024]{1,0:T(8,128)(2,1)S(1)} %copy-done, bf16[5,64,2,1024]{3,1,2,0:T(8,128)(2,1)} %copy-done.14, f32[5,64,2,1024]{3,1,2,0:T(8,128)} %fusion.12, f32[5,64,2,1024]{3,1,2,0:T(8,128)} %fusion.14, f32[5,64,2,1024]{3,1,2,0:T(8,128)} %fusion.16, f32[5,64,2,1024]{3,1,2,0:T(8,128)} %fusion.18, ...), kind=kOutput, calls=%fused_computation.33 | convolution fusion | flops 2694840320 | bytes 23068700 | tf_op jit(solution)/shard_map/...tc,cd->...td/dot_general | solution.py:35
  307.2 1.9 copy.32
  309.2 0.5 maximum_convert_fusion
  309.7 0.3 slice.159
  309.9 0.1 convert_multiply_fusion.2
  310.0 0.5 copy-done.11
  310.5 0.4 copy-done.13
  311.0 0.9 copy-done.2
  311.9 0.4 copy-done.5
  312.3 0.4 copy-done.8
  312.7 11.0 %fusion.5 = f32[5,64,2048]{2,1,0:T(8,128)S(1)} fusion(f32[5,64,2048]{2,1,0:T(8,128)S(1)} %bitcast.88, f32[5,64,2048]{2,1,0:T(8,128)S(1)} %slice.159, f32[5,1,2048]{2,1,0:T(1,128)S(1)} %get-tuple-element.7, f32[5,1,2048]{2,1,0:T(1,128)S(1)} %get-tuple-element.6, f32[5,64,2048]{2,1,0:T(8,128)S(1)} %bitcast.87, f32[]{:T(128)} %bitcast.13, f32[]{:T(128)} %bitcast.12, ...), kind=kLoop, calls=%fused_computation.11 | loop fusion | flops 19005440 | bytes 19743004 | tf_op jit(solution)/shard_map/sub | solution.py:106
  323.7 0.1 slice_reduce_fusion
  323.8 0.9 fusion.49
  (46 shorter events, 0.4 us)
Async XLA Ops:
  0.0 226.1 %copy-start = (bf16[1024,1024]{1,0:T(8,128)(2,1)S(1)}, bf16[1024,1024]{1,0:T(8,128)(2,1)}, u32[]{:S(2)}) copy-start(bf16[1024,1024]{1,0:T(8,128)(2,1)} %param.17) | copy-start | bytes 6291460
  0.0 6.9 %copy-start.18 = (s32[4096]{0:T(1024)S(1)}, s32[4096]{0:T(1024)}, u32[]{:S(2)}) copy-start(s32[4096]{0:T(1024)} %param.20) | copy-start | bytes 49156
  38.1 2.5 copy-start.16
  38.1 2.5 copy-start.17
  40.9 4.5 %collective-permute-start.1 = (bf16[5,1,2048]{2,1,0:T(2,128)(2,1)S(1)}, bf16[5,1,2048]{2,1,0:T(2,128)(2,1)}, u32[]{:S(2)}, u32[]{:S(2)}) collective-permute-start(bf16[5,1,2048]{2,1,0:T(2,128)(2,1)S(1)} %get-tuple-element.11), channel_id=1, source_target_pairs={{1,0},{2,1},{3,2},{4,3},{5,4},{6,5},{7,6},{8,7},{9,8},{10,9},{11,1... | collective-permute-start | bytes 61448 | tf_op jit(solution)/shard_map/ppermute | solution.py:19
  40.9 6.2 %collective-permute-start = (bf16[5,1,2048]{2,1,0:T(2,128)(2,1)S(1)}, bf16[5,1,2048]{2,1,0:T(2,128)(2,1)S(1)}, u32[]{:S(2)}, u32[]{:S(2)}) collective-permute-start(bf16[5,1,2048]{2,1,0:T(2,128)(2,1)S(1)} %get-tuple-element.10), channel_id=1, source_target_pairs={{0,1},{1,2},{2,3},{3,4},{4,5},{5,6},{6,7},{7,8},{8,9},{9,10},{10,1... | collective-permute-start | bytes 61448 | tf_op jit(solution)/shard_map/ppermute | solution.py:17
  43.6 137.7 %copy-start.15 = (bf16[4,64,2048]{2,1,0:T(8,128)(2,1)S(1)}, bf16[4,64,2048]{2,1,0:T(8,128)(2,1)}, u32[]{:S(2)}) copy-start(bf16[4,64,2048]{2,1,0:T(8,128)(2,1)} %get-tuple-element.20) | copy-start | bytes 3145732
  47.6 34.8 %collective-permute-start.2 = (bf16[5,66,2048]{2,1,0:T(8,128)(2,1)S(1)}, bf16[5,66,2048]{2,1,0:T(8,128)(2,1)S(1)}, u32[]{:S(2)}, u32[]{:S(2)}) collective-permute-start(bf16[5,66,2048]{2,1,0:T(8,128)(2,1)S(1)} %pad_maximum_fusion.2), channel_id=1, source_target_pairs={{14,0},{15,1},{0,2},{1,3},{2,4},{3,5},{4,6},{5,7},{6,8},{7,9},{8,1... | collective-permute-start | bytes 4055048 | tf_op jit(solution)/shard_map/ppermute | solution.py:29
  82.4 1.1 copy-start.3
  83.6 32.1 %collective-permute-start.3 = (bf16[5,66,2048]{2,1,0:T(8,128)(2,1)S(1)}, bf16[5,66,2048]{2,1,0:T(8,128)(2,1)S(1)}, u32[]{:S(2)}, u32[]{:S(2)}) collective-permute-start(bf16[5,66,2048]{2,1,0:T(8,128)(2,1)S(1)} %collective-permute-done.2), channel_id=1, source_target_pairs={{14,0},{15,1},{0,2},{1,3},{2,4},{3,5},{4,6},{5,7},{6,8},{7,9},{8,1... | collective-permute-start | bytes 4055048 | tf_op jit(solution)/shard_map/ppermute | solution.py:29
  115.6 1.1 copy-start.6
  116.8 31.2 %collective-permute-start.4 = (bf16[5,66,2048]{2,1,0:T(8,128)(2,1)S(1)}, bf16[5,66,2048]{2,1,0:T(8,128)(2,1)S(1)}, u32[]{:S(2)}, u32[]{:S(2)}) collective-permute-start(bf16[5,66,2048]{2,1,0:T(8,128)(2,1)S(1)} %collective-permute-done.3), channel_id=1, source_target_pairs={{14,0},{15,1},{0,2},{1,3},{2,4},{3,5},{4,6},{5,7},{6,8},{7,9},{8,1... | collective-permute-start | bytes 4055048 | tf_op jit(solution)/shard_map/ppermute | solution.py:29
  148.0 1.2 copy-start.9
  149.2 32.0 %collective-permute-start.5 = (bf16[5,66,2048]{2,1,0:T(8,128)(2,1)S(1)}, bf16[5,66,2048]{2,1,0:T(8,128)(2,1)}, u32[]{:S(2)}, u32[]{:S(2)}) collective-permute-start(bf16[5,66,2048]{2,1,0:T(8,128)(2,1)S(1)} %collective-permute-done.4), channel_id=1, source_target_pairs={{14,0},{15,1},{0,2},{1,3},{2,4},{3,5},{4,6},{5,7},{6,8},{7,9},{8,1... | collective-permute-start | bytes 4055048 | tf_op jit(solution)/shard_map/ppermute | solution.py:29
  181.2 31.0 %collective-permute-start.6 = (bf16[5,66,2048]{2,1,0:T(8,128)(2,1)}, bf16[5,66,2048]{2,1,0:T(8,128)(2,1)}, u32[]{:S(2)}, u32[]{:S(2)}) collective-permute-start(bf16[5,66,2048]{2,1,0:T(8,128)(2,1)} %collective-permute-done.5), channel_id=1, source_target_pairs={{14,0},{15,1},{0,2},{1,3},{2,4},{3,5},{4,6},{5,7},{6,8},{7,9},{8,1... | collective-permute-start | bytes 4055048 | tf_op jit(solution)/shard_map/ppermute | solution.py:29
  212.2 30.7 %collective-permute-start.7 = (bf16[5,66,2048]{2,1,0:T(8,128)(2,1)}, bf16[5,66,2048]{2,1,0:T(8,128)(2,1)}, u32[]{:S(2)}, u32[]{:S(2)}) collective-permute-start(bf16[5,66,2048]{2,1,0:T(8,128)(2,1)} %collective-permute-done.6), channel_id=1, source_target_pairs={{14,0},{15,1},{0,2},{1,3},{2,4},{3,5},{4,6},{5,7},{6,8},{7,9},{8,1... | collective-permute-start | bytes 4055048 | tf_op jit(solution)/shard_map/ppermute | solution.py:29
  216.3 2.2 copy-start.14
  216.8 7.5 %copy-start.19 = (f32[128]{0:T(128)S(1)}, f32[128]{0:T(128)}, u32[]{:S(2)}) copy-start(f32[128]{0:T(128)} %param.21) | copy-start | bytes 1540
  226.1 3.1 copy-start.7
  229.6 3.0 copy-start.10
  243.0 30.6 %collective-permute-start.8 = (bf16[5,66,2048]{2,1,0:T(8,128)(2,1)}, bf16[5,66,2048]{2,1,0:T(8,128)(2,1)S(1)}, u32[]{:S(2)}, u32[]{:S(2)}) collective-permute-start(bf16[5,66,2048]{2,1,0:T(8,128)(2,1)} %collective-permute-done.7), channel_id=1, source_target_pairs={{14,0},{15,1},{0,2},{1,3},{2,4},{3,5},{4,6},{5,7},{6,8},{7,9},{8,1... | collective-permute-start | bytes 4055048 | tf_op jit(solution)/shard_map/ppermute | solution.py:29
  258.0 15.6 %copy-start.1 = (f32[5,2,8,8,1024]{4,3,1,2,0:T(8,128)S(1)}, f32[5,2,8,8,1024]{4,3,1,2,0:T(8,128)}, u32[]{:S(2)}) copy-start(f32[5,2,8,8,1024]{4,3,1,2,0:T(8,128)} %copy.33) | copy-start | bytes 7864324
  258.0 15.6 %copy-start.4 = (bf16[5,66,2048]{2,1,0:T(8,128)(2,1)S(1)}, bf16[5,66,2048]{2,1,0:T(8,128)(2,1)}, u32[]{:S(2)}) copy-start(bf16[5,66,2048]{2,1,0:T(8,128)(2,1)} %copy-done.3) | copy-start | bytes 4055044
  273.6 16.3 %copy-start.12 = (bf16[5,66,2048]{2,1,0:T(8,128)(2,1)}, bf16[5,66,2048]{2,1,0:T(8,128)(2,1)S(1)}, u32[]{:S(2)}) copy-start(bf16[5,66,2048]{2,1,0:T(8,128)(2,1)S(1)} %collective-permute-done.8) | copy-start | bytes 4055044
  281.3 27.8 %collective-permute-start.10 = (bf16[5,1,2048]{2,1,0:T(2,128)(2,1)}, bf16[5,1,2048]{2,1,0:T(2,128)(2,1)S(1)}, u32[]{:S(2)}, u32[]{:S(2)}) collective-permute-start(bf16[5,1,2048]{2,1,0:T(2,128)(2,1)} %get-tuple-element.9), channel_id=1, source_target_pairs={{1,0},{2,1},{3,2},{4,3},{5,4},{6,5},{7,6},{8,7},{9,8},{10,9},{11,1... | collective-permute-start | bytes 61448 | tf_op jit(solution)/shard_map/ppermute | solution.py:19
  289.9 19.2 %collective-permute-start.9 = (bf16[5,1,2048]{2,1,0:T(2,128)(2,1)S(1)}, bf16[5,1,2048]{2,1,0:T(2,128)(2,1)S(1)}, u32[]{:S(2)}, u32[]{:S(2)}) collective-permute-start(bf16[5,1,2048]{2,1,0:T(2,128)(2,1)S(1)} %get-tuple-element.8), channel_id=1, source_target_pairs={{0,1},{1,2},{2,3},{3,4},{4,5},{5,6},{6,7},{7,8},{8,9},{9,10},{10,1... | collective-permute-start | bytes 61448 | tf_op jit(solution)/shard_map/ppermute | solution.py:17
  309.1 1.4 copy-start.11
  309.2 1.8 copy-start.13
  309.6 2.3 copy-start.2
  309.6 2.7 copy-start.5
  309.6 3.1 copy-start.8
where the time goes:
time: 326 us; the launch traced here: 325 us
  waiting for transfers between devices  183 us (56%)
  local copies, waits for them, and re-layouts  58.6 us (18%)
  matrix products  37.8 us (12%)
  other arithmetic  26.7 us (8%)
  starting transfers between devices  13.9 us (4%)
  between operations  4.94 us (2%)
    ppermute x7, waiting for transfers between devices, from_behind(): return lax.ppermute(block, axis, route)  180 us
    dot_general x8, matrix products, tile_apply(): jnp.einsum('...tc,cd->...td', shaped, matrix, preferred_element_type=jnp....  37.8 us
    scatter x1, local copies, waits for them, and re-layouts, on_device(): jnp.zeros((rows * columns,), jnp.bfloat16).at[offsets].set(1, mode='drop')  28.7 us
    sub x1, other arithmetic, on_device(): -divergence - weight_rows[None, :, None] * (wiener_wide * total_src)  11 us
    slice x7, local copies, waits for them, and re-layouts, on_device(): middle = moving[:, 1:-1]  8.88 us
    ppermute x2, starting transfers between devices, extended(): lax.ppermute(head, axis, [((i + 1) % count, i) for i in range(count)])  8.67 us
    convert_element_type x1, other arithmetic, on_device(): flux_dec.astype(jnp.bfloat16)  7.01 us
  transfers between devices with their start and end apart: 11, of which 9 were waited for; matrix products, arithmetic and copies ran while one was open for 17% of the time, Pallas kernels for 0%

commit v1 on v0

v1 whole, which is shorter than its diff:
```python
import functools

import jax
import jax.numpy as jnp
from jax import lax
from jax.experimental import pallas as pl
from jax.experimental.pallas import tpu as pltpu
from jax.sharding import PartitionSpec as P

PIECES = 2
MESH = pl.DeviceIdType.MESH


def tile_apply(values, matrix):
    width = matrix.shape[0]
    shaped = values.reshape(values.shape[:-1] + (values.shape[-1] // width, width))
    result = jnp.einsum("...tc,cd->...td", shaped, matrix, preferred_element_type=jnp.float32)
    return result.reshape(values.shape)


def pair_sums(nsplit, pair_ref, x_ref, s_ref, ro, r1, r2, ra, rb, yb, pa, pb, bb, send, recv):
    count = x_ref.shape[0]
    group = lax.axis_size("sim") // nsplit
    index = lax.axis_index("sim")
    place = index // group
    lane = index % group
    levels = nsplit // 2
    level = place // 2
    column = place % 2
    back = (lane < group // 2).astype(jnp.int32)
    low = level < levels // 2
    is_outer = (level == 0) | (level == levels - 1)

    def at(lev, col):
        return lev * 2 + col

    def device(pos):
        return {"sim": pos * group + lane}

    def weight(dest, source):
        row = (dest - back + nsplit) % nsplit
        col = (source - back + nsplit) % nsplit
        value = pair_ref[row, col].astype(jnp.float32)
        return value * (dest != source).astype(jnp.float32)

    other = 1 - column
    partner = at(level, other)
    near_outer = jnp.where(low, 0, levels - 1)
    near_inner = jnp.where(low, 1, levels - 2)
    far_inner = jnp.where(low, levels - 2, 1)
    far_outer = jnp.where(low, levels - 1, 0)

    def copy(stream, n, src, dst, pos):
        return pltpu.make_async_remote_copy(
            src_ref=src.at[n], dst_ref=dst.at[n],
            send_sem=send.at[stream, n], recv_sem=recv.at[stream, n],
            device_id=device(pos), device_id_type=MESH,
        )

    barrier = pltpu.get_barrier_semaphore()

    def greet(pos):
        pl.semaphore_signal(barrier, inc=1, device_id=device(pos), device_id_type=MESH)

    def wide(ref, n):
        return ref[n].astype(jnp.float32)

    def across(n):
        return copy(5, n, bb, yb, partner)

    def finish(n):
        across(n).wait_recv()
        s_ref[n] = s_ref[n] + wide(yb, n)

    @pl.when(is_outer)
    def _():
        inner = at(near_inner, column)
        greet(inner)
        greet(partner)
        pl.semaphore_wait(barrier, 2)

        def give(n):
            return copy(0, n, x_ref, ro, inner)

        @pl.loop(0, count)
        def _(n):
            give(n).start()

        own = weight(partner, place)

        @pl.loop(0, count)
        def _(n):
            copy(4, n, pb, rb, inner).wait_recv()
            bb[n] = (wide(rb, n) + own * wide(x_ref, n)).astype(bb.dtype)
            across(n).start()
            copy(3, n, pa, ra, inner).wait_recv()
            s_ref[n] = wide(ra, n)

        @pl.loop(0, count)
        def _(n):
            finish(n)
            give(n).wait_send()
            across(n).wait_send()

    @pl.when(jnp.logical_not(is_outer))
    def _():
        outer = at(near_outer, column)
        far = at(far_inner, column)
        edge = at(far_outer, column)
        greet(outer)
        greet(far)
        greet(partner)
        pl.semaphore_wait(barrier, 3)

        def own(n):
            return copy(1, n, x_ref, r1, far)

        def relay(n):
            return copy(2, n, ro, r2, far)

        def to_a(n):
            return copy(3, n, pa, ra, outer)

        def to_b(n):
            return copy(4, n, pb, rb, outer)

        def forward(n):
            own(n).start()
            copy(0, n, x_ref, ro, outer).wait_recv()
            relay(n).start()

        @pl.loop(0, 2)
        def _(n):
            forward(n)

        outer_other = at(near_outer, other)
        a_own, a_far, a_edge = weight(outer, place), weight(outer, far), weight(outer, edge)
        b_own, b_far, b_edge = weight(outer_other, place), weight(outer_other, far), weight(outer_other, edge)
        y_own, y_out = weight(partner, place), weight(partner, outer)
        y_far, y_edge = weight(partner, far), weight(partner, edge)
        s_out, s_far, s_edge = weight(place, outer), weight(place, far), weight(place, edge)

        @pl.loop(0, count)
        def _(n):
            @pl.when(n + 2 < count)
            def _():
                forward(n + 2)

            own(n).wait_recv()
            relay(n).wait_recv()
            mine, out, far_v, edge_v = wide(x_ref, n), wide(ro, n), wide(r1, n), wide(r2, n)
            pa[n] = (a_own * mine + a_far * far_v + a_edge * edge_v).astype(pa.dtype)
            pb[n] = (b_own * mine + b_far * far_v + b_edge * edge_v).astype(pb.dtype)
            to_b(n).start()
            to_a(n).start()
            bb[n] = (y_own * mine + y_out * out + y_far * far_v + y_edge * edge_v).astype(bb.dtype)
            across(n).start()
            s_ref[n] = s_out * out + s_far * far_v + s_edge * edge_v

        @pl.loop(0, count)
        def _(n):
            finish(n)
            own(n).wait_send()
            relay(n).wait_send()
            to_a(n).wait_send()
            to_b(n).wait_send()
            across(n).wait_send()


def gather_sums(chosen, pair_table):
    fields, rows, columns = chosen.shape
    nsplit = pair_table.shape[0]
    shape = (fields * PIECES, rows // PIECES, columns)
    buffer = pltpu.VMEM(shape, chosen.dtype)
    sums = pl.pallas_call(
        functools.partial(pair_sums, nsplit),
        out_shape=jax.ShapeDtypeStruct(shape, jnp.float32),
        in_specs=[pl.BlockSpec(memory_space=pltpu.SMEM), pl.BlockSpec(memory_space=pltpu.VMEM)],
        out_specs=pl.BlockSpec(memory_space=pltpu.VMEM),
        scratch_shapes=[buffer] * 9
        + [pltpu.SemaphoreType.DMA((6, shape[0])), pltpu.SemaphoreType.DMA((6, shape[0]))],
        compiler_params=pltpu.CompilerParams(
            collective_id=0, has_side_effects=True, vmem_limit_bytes=48 << 20
        ),
    )(pair_table, chosen.reshape(shape))
    return sums.reshape(fields, rows, columns)


def rims(cells, band_index, group_bands):
    count = lax.axis_size("sim")
    below = lax.ppermute(cells[:, -1:], "sim", [(i, (i + 1) % count) for i in range(count)])
    above = lax.ppermute(cells[:, :1], "sim", [((i + 1) % count, i) for i in range(count)])
    below = below * (band_index > 0).astype(cells.dtype)
    above = above * (band_index < group_bands - 1).astype(cells.dtype)
    return jnp.concatenate([below, cells, above], axis=1)


def row_slope(padded):
    return (padded[:, 2:] - padded[:, :-2]) * 0.5


def on_device(
    sky_maps,
    ivf_maps,
    sim_sky,
    sim_ivf,
    ra_wiener,
    ra_gradient,
    pair_table,
    sim_index,
    source_pixels,
    response,
):
    nsplit = pair_table.shape[0]
    nuse = sim_index.shape[0]
    axis_count = lax.axis_size("sim")
    group_bands = axis_count // nsplit
    logical = (lax.axis_index("sim") - group_bands // 2) % axis_count
    band_index = logical % group_bands
    rows, columns = sky_maps.shape
    chosen_sky = jnp.concatenate([sky_maps[None], jnp.take(sim_sky, sim_index, axis=0)], axis=0)
    chosen_ivf = jnp.concatenate([ivf_maps[None], jnp.take(sim_ivf, sim_index, axis=0)], axis=0)
    sums = gather_sums(chosen_ivf, pair_table)
    offsets = source_pixels - band_index * rows * columns
    inside = (offsets >= 0) & (offsets < rows * columns)
    offsets = jnp.where(inside, offsets, rows * columns)
    hit = jnp.zeros((rows * columns,), jnp.float32).at[offsets].set(1, mode="drop")
    keep = (1 - hit).reshape(rows, columns)
    sums = sums * keep[None]
    wiener = tile_apply(chosen_sky, ra_wiener).astype(jnp.bfloat16).astype(jnp.float32)
    total_ra = tile_apply(sums.astype(jnp.bfloat16), ra_gradient)
    total_dec = row_slope(rims(sums, band_index, group_bands))
    flux_ra = (wiener * total_ra).astype(jnp.bfloat16).astype(jnp.float32)
    flux_dec = wiener * total_dec
    flux_src = wiener * sums

    def combine(values):
        return values[:1] - jnp.sum(values[1:], axis=0, keepdims=True) / nuse

    divergence = tile_apply(combine(flux_ra).astype(jnp.bfloat16), ra_gradient)
    divergence = divergence + row_slope(rims(combine(flux_dec), band_index, group_bands))
    weight_rows = lax.dynamic_slice_in_dim(response, band_index * rows, rows)
    return (-divergence - weight_rows[None, :, None] * combine(flux_src))[0]


def solution(mesh):
    in_specs = (
        P(("patch", "sim"), None),
        P(("patch", "sim"), None),
        P(None, ("patch", "sim"), None),
        P(None, ("patch", "sim"), None),
        P(),
        P(),
        P(),
        P(),
        P("patch"),
        P("patch"),
    )
    out_specs = P(("patch", "sim"), None)
    return jax.shard_map(
        on_device, mesh=mesh, in_specs=in_specs, out_specs=out_specs, check_vma=False
    )
```

time: 326 us -> 144 us (0.44)
  the two profiles are of different devices: /device:TPU:1 before, /device:TPU:0 now
where the time goes in v1:
time: 144 us; the launch traced here: 143 us
  Pallas kernels  74.9 us (52%)
  local copies, waits for them, and re-layouts  39.5 us (27%)
  other arithmetic  14.8 us (10%)
  matrix products  8.09 us (6%)
  starting transfers between devices  4.62 us (3%)
    pallas_call x1, Pallas kernels, gather_sums(): pl.pallas_call(functools.partial(pair_sums, nsplit), out_shape=jax.ShapeD...  74.9 us
    scatter x1, local copies, waits for them, and re-layouts, on_device(): jnp.zeros((rows * columns,), jnp.float32).at[offsets].set(1, mode='drop')  15.7 us
    dot_general x3, matrix products, tile_apply(): jnp.einsum('...tc,cd->...td', shaped, matrix, preferred_element_type=jnp....  8.09 us
    reshape x2, local copies, waits for them, and re-layouts, tile_apply(): return result.reshape(values.shape)  5.92 us
    mul x1, other arithmetic, on_device(): flux_dec = wiener * total_dec  5.33 us
    reshape x1, local copies, waits for them, and re-layouts, gather_sums(): return sums.reshape(fields, rows, columns)  4.85 us
    ppermute x2, starting transfers between devices, rims(): lax.ppermute(cells[:, :1], 'sim', [((i + 1) % count, i) for i in range(co...  4.12 us
    gather x1, local copies, waits for them, and re-layouts, on_device(): jnp.take(sim_sky, sim_index, axis=0)  3.23 us
  transfers between devices with their start and end apart: 4, of which 1 were waited for; matrix products, arithmetic and copies ran while one was open for 13% of the time, Pallas kernels for 0%

profile of v1, /device:TPU:0, one launch (start us, length us, event | category | flops | bytes accessed | tf_op | source)
XLA Modules:
  0.0 143.0 jit_solution(4963647720423434037)
XLA Ops:
  0.0 0.0 copy-start
  0.0 0.8 compare_and_fusion
  0.8 0.7 compare_select_fusion.1
  1.5 1.1 concatenate.25
  2.7 0.7 compare_select_fusion
  3.4 15.7 %scatter_custom_fusion = f32[131072]{0:T(1024)S(1)} fusion(s32[4096]{0:T(1024)S(1)} %compare_select_fusion, f32[4096]{0:T(1024)S(1)} %broadcast.64, f32[]{:T(128)} %constant.27.clone.1), kind=kCustom, calls=%fused_computation.47 | custom fusion | bytes 524292 | tf_op jit(solution)/shard_map/scatter | solution.py:227
  19.1 0.1 mul.82
  19.2 3.2 %gather_fusion.1 = bf16[4,64,2048]{2,1,0:T(8,128)(2,1)} fusion(bf16[8,64,2048]{2,1,0:T(8,128)(2,1)} %param.15, s32[1024]{0:T(1024)S(1)} %pad_clamp_fusion), kind=kCustom, calls=%fused_computation.1.clone | custom fusion | bytes 2097168 | tf_op jit(solution)/shard_map/jit(_take)/gather | solution.py:222
  22.4 3.2 %gather_fusion = bf16[4,64,2048]{2,1,0:T(8,128)(2,1)} fusion(bf16[8,64,2048]{2,1,0:T(8,128)(2,1)} %param.14, s32[1024]{0:T(1024)S(1)} %pad_clamp_fusion), kind=kCustom, calls=%fused_computation.clone | custom fusion | bytes 2097168 | tf_op jit(solution)/shard_map/jit(_take)/gather | solution.py:221
  25.6 0.0 copy-start.7
  25.6 1.9 %broadcast_select_fusion = (bf16[4,64,2048]{2,1,0:T(8,128)(2,1)S(1)}, bf16[4,64,2048]{2,1,0:T(8,128)(2,1)S(1)}) fusion(bf16[4,64,2048]{2,1,0:T(8,128)(2,1)} %gather_fusion.1, pred[4]{0:T(512)(128)(4,1)S(1)} %compare_and_fusion, bf16[4,64,2048]{2,1,0:T(8,128)(2,1)} %gather_fusion), kind=kLoop, calls=%fused_computation.31 | loop fusion | flops 1048576 | bytes 4194308 | tf_op jit(solution)/shard_map/jit(_take)/select_n | solution.py:222
  27.6 0.1 copy.33
  27.7 0.2 copy-done.7
  27.9 1.5 %convert_bitcast_fusion = f32[5,2,8,8,1024]{4,3,2,1,0:T(8,128)S(1)} fusion(bf16[1024,1024]{1,0:T(8,128)(2,1)S(1)} %copy-done.7, bf16[4,64,2,1024]{3,1,2,0:T(8,128)(2,1)S(1)} %bitcast.49, bf16[1,64,2,1024]{3,1,2,0:T(8,128)(2,1)S(1)} %copy.13), kind=kOutput, calls=%fused_computation.11 | convolution fusion | flops 1344143360 | bytes 6029312 | tf_op jit(solution)/shard_map/...tc,cd->...td/dot_general | solution.py:17
  29.4 0.0 copy-start.6
  29.4 0.3 copy.24
  29.7 0.0 copy-start.3
  29.7 0.0 copy-start.2
  29.7 0.6 copy-done.6
  30.3 0.1 pad_maximum_fusion.2
  30.5 0.0 copy-done.2
  30.5 74.9 %shard_map.100 = f32[10,32,2048]{2,1,0:T(8,128)S(1)} custom-call(s32[8,8]{1,0:T(8,128)S(1)} %copy-done.2, bf16[10,32,2048]{2,1,0:T(8,128)(2,1)S(1)} %bitcast.44), custom_call_target="tpu_custom_call" | custom-call | tf_op jit(solution)/shard_map/pallas_call | solution.py:175
  105.4 0.0 copy-start.1
  105.4 0.0 copy-done.3
  105.4 2.3 %fusion.36 = (f32[5,64,2048]{2,1,0:T(8,128)}, f32[5,64,2048]{2,1,0:T(8,128)S(1)}) fusion(f32[5,64,2048]{2,1,0:T(8,128)S(1)} %bitcast.45, f32[64,2048]{1,0:T(8,128)S(1)} %mul.82, f32[5,64,2048]{2,1,0:T(8,128)S(1)} %bitcast.43), kind=kLoop, calls=%fused_computation.59 | loop fusion | flops 1310720 | bytes 11010048 | tf_op jit(solution)/shard_map/mul | solution.py:235
  107.7 0.0 copy-done.1
  107.7 0.0 copy-start.4
  107.7 1.5 %copy-done.4 = f32[5,64,2048]{2,1,0:T(8,128)} copy-done((f32[5,64,2048]{2,1,0:T(8,128)}, f32[5,64,2048]{2,1,0:T(8,128)S(1)}, u32[]{:S(2)}) %copy-start.4) | copy-done | bytes 2621464
  109.1 0.1 fusion.37
  109.2 0.1 collective-permute-start
  109.3 0.5 collective-permute-start.1
  109.8 0.3 mul.78
  110.0 4.9 %reshape.73 = f32[5,64,2,1024]{3,2,1,0:T(2,128)} reshape(f32[10,32,2048]{2,1,0:T(8,128)} %copy-done.1) | data formatting | bytes 5242880 | tf_op jit(solution)/shard_map/reshape | solution.py:186
  114.9 0.2 copy.16
  115.1 0.0 copy-done
  115.1 0.0 copy-start.5
  115.1 5.2 %fusion.10 = f32[5,2,8,8,1024]{4,3,2,1,0:T(8,128)} fusion(bf16[1024,1024]{1,0:T(8,128)(2,1)S(1)} %copy-done, f32[5,64,2,1024]{3,2,1,0:T(2,128)} %reshape.73, f32[64,2,1024]{2,0,1:T(8,128)S(1)} %copy.16), kind=kOutput, calls=%fused_computation.22 | convolution fusion | flops 1343488000 | bytes 7864320 | tf_op jit(solution)/shard_map/...tc,cd->...td/dot_general | solution.py:17
  120.3 0.0 copy-done.5
  120.3 0.1 slice_reduce_fusion
  120.4 0.0 copy-start.8
  120.4 3.6 %copy.25 = f32[5,2,8,8,1024]{4,3,1,2,0:T(8,128)} copy(f32[5,2,8,8,1024]{4,3,2,1,0:T(8,128)} %fusion.10) | data formatting | bytes 5242880 | tf_op jit(solution)/shard_map/reshape | solution.py:18
  124.0 0.0 copy-done.8
  124.0 0.1 dynamic_slice.3
  124.1 0.0 collective-permute-done
  124.2 0.0 collective-permute-done.1
  124.2 5.3 %fusion.2 = (f32[5,64,2048]{2,1,0:T(8,128)S(1)}, f32[5,64,2048]{2,1,0:T(8,128)S(1)}) fusion(f32[5,64,2048]{2,1,0:T(8,128)} %bitcast.46, f32[5,64,2048]{2,1,0:T(8,128)} %copy-done.4, f32[5,1,2048]{2,1,0:T(1,128)S(1)} %broadcast_multiply_fusion, f32[5,1,2048]{2,1,0:T(1,128)S(1)} %broadcast_multiply_fusion.1, f32[5,64,2048]{2,1,0:T(8,128)} %bitcast.47), kind=kLoop, calls=%fused_computation.6 | loop fusion | flops 5242880 | bytes 13189120 | tf_op jit(solution)/shard_map/mul | solution.py:234
  129.5 0.4 slice_reduce_fusion.1
  129.9 0.1 fusion.31
  130.0 0.1 slice_subtract_fusion.1
  130.1 0.9 reshape.75
  131.0 4.1 %collective-permute-start.2 = (f32[1,1,2048]{2,1,0:T(1,128)S(1)}, f32[1,1,2048]{2,1,0:T(1,128)S(1)}, u32[]{:S(2)}, u32[]{:S(2)}) collective-permute-start(f32[1,1,2048]{2,1,0:T(1,128)S(1)} %get-tuple-element.12), channel_id=1, source_target_pairs={{1,0},{2,1},{3,2},{4,3},{5,4},{6,5},{7,6},{8,7},{9,8},{10,9},{11,1... | collective-permute-start | bytes 24584 | tf_op jit(solution)/shard_map/ppermute | solution.py:192
  135.0 0.0 collective-permute-start.3
  135.0 1.4 fusion.8
  136.4 1.2 copy.20
  137.6 2.3 %reshape.76 = f32[1,64,2048]{2,1,0:T(8,128)} reshape(f32[64,2,1024]{2,1,0:T(2,128)} %copy.20) | data formatting | bytes 1048576 | tf_op jit(solution)/shard_map/reshape | solution.py:18
  139.9 0.0 collective-permute-done.2
  139.9 0.9 collective-permute-done.3
  140.8 2.2 %fusion.26 = f32[64,2048]{1,0:T(8,128)} fusion(f32[5,64,2048]{2,1,0:T(8,128)} %get-tuple-element.6, f32[1,64,2048]{2,1,0:T(8,128)} %reshape.76, f32[1,64,2048]{2,1,0:T(8,128)S(1)} %slice_subtract_fusion.1, f32[1,1,2048]{2,1,0:T(1,128)S(1)} %broadcast_multiply_fusion.2, f32[1,1,2048]{2,1,0:T(1,128)S(1)} %broadcast_multiply_fusion.3, ...), kind=kLoop, calls=%fused_computation.36 | loop fusion | flops 1310720 | bytes 2638080 | tf_op jit(solution)/shard_map/squeeze | solution.py:243
  (9 shorter events, 0.2 us)
Async XLA Ops:
  0.0 115.1 %copy-start = (bf16[1024,1024]{1,0:T(8,128)(2,1)S(1)}, bf16[1024,1024]{1,0:T(8,128)(2,1)}, u32[]{:S(2)}) copy-start(bf16[1024,1024]{1,0:T(8,128)(2,1)} %param.17) | copy-start | bytes 6291460
  25.6 2.2 %copy-start.7 = (bf16[1024,1024]{1,0:T(8,128)(2,1)S(1)}, bf16[1024,1024]{1,0:T(8,128)(2,1)}, u32[]{:S(2)}) copy-start(bf16[1024,1024]{1,0:T(8,128)(2,1)} %param.16) | copy-start | bytes 6291460
  29.4 1.0 copy-start.6
  29.7 75.7 %copy-start.3 = (f32[5,2,8,8,1024]{4,3,1,2,0:T(8,128)}, f32[5,2,8,8,1024]{4,3,1,2,0:T(8,128)S(1)}, u32[]{:S(2)}) copy-start(f32[5,2,8,8,1024]{4,3,1,2,0:T(8,128)S(1)} %copy.24) | copy-start | bytes 7864324
  29.7 0.7 copy-start.2
  105.4 2.3 %copy-start.1 = (f32[10,32,2048]{2,1,0:T(8,128)}, f32[10,32,2048]{2,1,0:T(8,128)S(1)}, u32[]{:S(2)}) copy-start(f32[10,32,2048]{2,1,0:T(8,128)S(1)} %shard_map.100) | copy-start | bytes 7864324
  107.7 1.5 %copy-start.4 = (f32[5,64,2048]{2,1,0:T(8,128)}, f32[5,64,2048]{2,1,0:T(8,128)S(1)}, u32[]{:S(2)}) copy-start(f32[5,64,2048]{2,1,0:T(8,128)S(1)} %get-tuple-element.7) | copy-start | bytes 7864324
  109.2 14.9 %collective-permute-start = (f32[5,1,2048]{2,1,0:T(1,128)S(1)}, f32[5,1,2048]{2,1,0:T(1,128)S(1)}, u32[]{:S(2)}, u32[]{:S(2)}) collective-permute-start(f32[5,1,2048]{2,1,0:T(1,128)S(1)} %get-tuple-element.10), channel_id=1, source_target_pairs={{1,0},{2,1},{3,2},{4,3},{5,4},{6,5},{7,6},{8,7},{9,8},{10,9},{11,1... | collective-permute-start | bytes 122888 | tf_op jit(solution)/shard_map/ppermute | solution.py:192
  109.3 14.9 %collective-permute-start.1 = (f32[5,1,2048]{2,1,0:T(1,128)S(1)}, f32[5,1,2048]{2,1,0:T(1,128)S(1)}, u32[]{:S(2)}, u32[]{:S(2)}) collective-permute-start(f32[5,1,2048]{2,1,0:T(1,128)S(1)} %get-tuple-element.11), channel_id=1, source_target_pairs={{0,1},{1,2},{2,3},{3,4},{4,5},{5,6},{6,7},{7,8},{8,9},{9,10},{10,1... | collective-permute-start | bytes 122888 | tf_op jit(solution)/shard_map/ppermute | solution.py:191
  115.1 5.2 %copy-start.5 = (f32[5,64,2048]{2,1,0:T(8,128)S(1)}, f32[5,64,2048]{2,1,0:T(8,128)}, u32[]{:S(2)}) copy-start(f32[5,64,2048]{2,1,0:T(8,128)} %get-tuple-element.6) | copy-start | bytes 7864324
  120.4 3.6 %copy-start.8 = (f32[128]{0:T(128)S(1)}, f32[128]{0:T(128)}, u32[]{:S(2)}) copy-start(f32[128]{0:T(128)} %param.21) | copy-start | bytes 1540
  131.0 9.0 %collective-permute-start.2 = (f32[1,1,2048]{2,1,0:T(1,128)S(1)}, f32[1,1,2048]{2,1,0:T(1,128)S(1)}, u32[]{:S(2)}, u32[]{:S(2)}) collective-permute-start(f32[1,1,2048]{2,1,0:T(1,128)S(1)} %get-tuple-element.12), channel_id=1, source_target_pairs={{1,0},{2,1},{3,2},{4,3},{5,4},{6,5},{7,6},{8,7},{9,8},{10,9},{11,1... | collective-permute-start | bytes 24584 | tf_op jit(solution)/shard_map/ppermute | solution.py:192
  135.0 5.8 %collective-permute-start.3 = (f32[1,1,2048]{2,1,0:T(1,128)S(1)}, f32[1,1,2048]{2,1,0:T(1,128)S(1)}, u32[]{:S(2)}, u32[]{:S(2)}) collective-permute-start(f32[1,1,2048]{2,1,0:T(1,128)S(1)} %get-tuple-element.13), channel_id=1, source_target_pairs={{0,1},{1,2},{2,3},{3,4},{4,5},{5,6},{6,7},{7,8},{8,9},{9,10},{10,1... | collective-permute-start | bytes 24584 | tf_op jit(solution)/shard_map/ppermute | solution.py:191

commit v2 on v1

v2 whole, which is shorter than its diff:
```python
import functools

import jax
import jax.numpy as jnp
from jax import lax
from jax.experimental import pallas as pl
from jax.experimental.pallas import tpu as pltpu
from jax.sharding import PartitionSpec as P

PIECES = 2
LANES = 128
SLAB = 8
MESH = pl.DeviceIdType.MESH


def pick(index_ref, maps_a, maps_b, sim_a, sim_b, out_a, out_b):
    @pl.when(pl.program_id(0) == 0)
    def _():
        out_a[0] = maps_a[...]
        out_b[0] = maps_b[...]

    @pl.when(pl.program_id(0) > 0)
    def _():
        out_a[...] = sim_a[...]
        out_b[...] = sim_b[...]


def choose(sim_index, maps_a, maps_b, sim_a, sim_b):
    rows, columns = maps_a.shape
    fields = sim_index.shape[0] + 1
    whole = pl.BlockSpec((rows, columns), lambda f, ids: (0, 0))
    picked = pl.BlockSpec((1, rows, columns), lambda f, ids: (ids[jnp.maximum(f - 1, 0)], 0, 0))
    placed = pl.BlockSpec((1, rows, columns), lambda f, ids: (f, 0, 0))
    shape = jax.ShapeDtypeStruct((fields, rows, columns), maps_a.dtype)
    return pl.pallas_call(
        pick,
        grid_spec=pltpu.PrefetchScalarGridSpec(
            num_scalar_prefetch=1, grid=(fields,),
            in_specs=[whole, whole, picked, picked], out_specs=[placed, placed],
        ),
        out_shape=[shape, shape],
    )(sim_index, maps_a, maps_b, sim_a, sim_b)


def estimator(
    nsplit, pair_ref, x_ref, sky_ref, wiener_ref, grad_ref, key_ref, lane_ref, resp_ref, out_ref,
    ro, r1, r2, ra, rb, yb, pa, pb, bb, sums, keep, sm, wf, acc_f, acc_d, acc_s,
    up_w, dn_w, bl_w, ab_w, up_e, dn_e, bl_e, ab_e, send, recv, slab_send, slab_recv,
):
    count = x_ref.shape[0]
    fields, rows, columns = sky_ref.shape
    part = rows // PIECES
    width = grad_ref.shape[0]
    tiles = columns // width
    f32, bf16 = jnp.float32, jnp.bfloat16
    devices = lax.axis_size("sim")
    group = devices // nsplit
    index = lax.axis_index("sim")
    place = index // group
    lane = index % group
    band = (lane - group // 2 + group) % group
    levels = nsplit // 2
    level = place // 2
    column = place % 2
    back = (lane < group // 2).astype(jnp.int32)
    low = level < levels // 2
    is_outer = (level == 0) | (level == levels - 1)
    is_inner = jnp.logical_not(is_outer)
    has_above = band < group - 1
    has_below = band > 0

    def at(lev, col):
        return lev * 2 + col

    def device(pos):
        return {"sim": pos * group + lane}

    def weight(dest, source):
        row = (dest - back + nsplit) % nsplit
        col = (source - back + nsplit) % nsplit
        value = pair_ref[row, col].astype(f32)
        return value * (dest != source).astype(f32)

    other = 1 - column
    partner = at(level, other)
    near_outer = jnp.where(low, 0, levels - 1)
    near_inner = jnp.where(low, 1, levels - 2)
    far_inner = jnp.where(low, levels - 2, 1)
    far_outer = jnp.where(low, levels - 1, 0)
    inner = at(near_inner, column)
    outer = at(near_outer, column)
    far = at(far_inner, column)
    edge = at(far_outer, column)
    above = {"sim": (index + 1) % devices}
    below = {"sim": (index + devices - 1) % devices}

    def copy(stream, n, src, dst, pos):
        return pltpu.make_async_remote_copy(
            src_ref=src.at[n], dst_ref=dst.at[n],
            send_sem=send.at[stream, n], recv_sem=recv.at[stream, n],
            device_id=device(pos), device_id_type=MESH,
        )

    def slab(which, src, dst, target):
        return pltpu.make_async_remote_copy(
            src_ref=src, dst_ref=dst,
            send_sem=slab_send.at[which], recv_sem=slab_recv.at[which],
            device_id=target, device_id_type=MESH,
        )

    wiener_up = slab(0, up_w, bl_w, above)
    wiener_down = slab(1, dn_w, ab_w, below)
    edge_up = slab(2, up_e, bl_e, above)
    edge_down = slab(3, dn_e, ab_e, below)

    def wide(ref, n):
        return ref[n].astype(f32)

    def across(n):
        return copy(5, n, bb, yb, partner)

    def give(n):
        return copy(0, n, x_ref, ro, inner)

    def own(n):
        return copy(1, n, x_ref, r1, far)

    def relay(n):
        return copy(2, n, ro, r2, far)

    def to_a(n):
        return copy(3, n, pa, ra, outer)

    def to_b(n):
        return copy(4, n, pb, rb, outer)

    def forward(n):
        own(n).start()
        copy(0, n, x_ref, ro, outer).wait_recv()
        relay(n).start()

    barrier = pltpu.get_barrier_semaphore()

    def greet(target):
        pl.semaphore_signal(barrier, inc=1, device_id=target, device_id_type=MESH)

    greet(device(partner))

    @pl.when(has_above)
    def _():
        greet(above)

    @pl.when(has_below)
    def _():
        greet(below)

    @pl.when(is_outer)
    def _():
        greet(device(inner))

    @pl.when(is_inner)
    def _():
        greet(device(outer))
        greet(device(far))

    met = 2 + is_inner.astype(jnp.int32) + has_above.astype(jnp.int32) + has_below.astype(jnp.int32)
    pl.semaphore_wait(barrier, met)

    @pl.when(is_outer)
    def _():
        @pl.loop(0, count)
        def _(n):
            give(n).start()

    @pl.when(is_inner)
    def _():
        @pl.loop(0, 2)
        def _(n):
            forward(n)

    acc_f[...] = jnp.zeros_like(acc_f)
    acc_d[...] = jnp.zeros_like(acc_d)
    acc_s[...] = jnp.zeros_like(acc_s)
    up_e[...] = jnp.zeros_like(up_e)
    dn_e[...] = jnp.zeros_like(dn_e)
    up_w[...] = jnp.zeros_like(up_w)
    dn_w[...] = jnp.zeros_like(dn_w)

    @pl.when(jnp.logical_not(has_above))
    def _():
        ab_w[...] = jnp.zeros_like(ab_w)
        ab_e[...] = jnp.zeros_like(ab_e)

    @pl.when(jnp.logical_not(has_below))
    def _():
        bl_w[...] = jnp.zeros_like(bl_w)
        bl_e[...] = jnp.zeros_like(bl_e)

    outer_other = at(near_outer, other)
    y_out_own = weight(partner, place)
    a_far, a_edge, a_own = weight(outer, far), weight(outer, edge), weight(outer, place)
    b_far, b_edge, b_own = weight(outer_other, far), weight(outer_other, edge), weight(outer_other, place)
    y_out, y_far, y_edge = weight(partner, outer), weight(partner, far), weight(partner, edge)
    s_out, s_far, s_edge = weight(place, outer), weight(place, far), weight(place, edge)

    def outer_piece(n):
        copy(4, n, pb, rb, inner).wait_recv()
        bb[n] = (wide(rb, n) + y_out_own * wide(x_ref, n)).astype(bf16)
        across(n).start()
        copy(3, n, pa, ra, inner).wait_recv()
        sums[n] = wide(ra, n)

    def inner_piece(n):
        @pl.when(n + 2 < count)
        def _():
            forward(n + 2)

        own(n).wait_recv()
        relay(n).wait_recv()
        mine, out, far_v, edge_v = wide(x_ref, n), wide(ro, n), wide(r1, n), wide(r2, n)
        pb[n] = (b_own * mine + b_far * far_v + b_edge * edge_v).astype(bf16)
        pa[n] = (a_own * mine + a_far * far_v + a_edge * edge_v).astype(bf16)
        to_b(n).start()
        to_a(n).start()
        bb[n] = (y_out_own * mine + y_out * out + y_far * far_v + y_edge * edge_v).astype(bf16)
        across(n).start()
        sums[n] = s_out * out + s_far * far_v + s_edge * edge_v

    def tile_dot(values):
        high = values.astype(bf16)
        rest = (values - high.astype(f32)).astype(bf16)
        lefts = [half[:, t * width:(t + 1) * width] for half in (high, rest) for t in range(tiles)]
        result = jnp.dot(jnp.concatenate(lefts, axis=0), grad_ref[...], preferred_element_type=f32)
        blocks = [
            result[t * rows:(t + 1) * rows] + result[(tiles + t) * rows:(tiles + t + 1) * rows]
            for t in range(tiles)
        ]
        return jnp.concatenate(blocks, axis=1)

    row_of = lax.broadcasted_iota(jnp.int32, (rows, columns), 0)

    def slope(values, before, after):
        upper = jnp.where(row_of == rows - 1, after, pltpu.roll(values, rows - 1, 0))
        lower = jnp.where(row_of == 0, before, pltpu.roll(values, 1, 0))
        return (upper - lower) * 0.5

    def share(f):
        return jnp.where(f == 0, jnp.float32(1.0), jnp.float32(-1.0 / (fields - 1)))

    def filter_sky(f):
        sky = sky_ref[f]
        lefts = [sky[:, t * width:(t + 1) * width] for t in range(tiles)]
        result = jnp.dot(jnp.concatenate(lefts, axis=0), wiener_ref[...], preferred_element_type=f32)
        result = result.astype(bf16).astype(f32)
        for t in range(tiles):
            wf[f, :, t * width:(t + 1) * width] = result[t * rows:(t + 1) * rows]
        up_w[pl.ds(f, 1), :] = wf[f, rows - 1:rows, :]
        dn_w[pl.ds(f, 1), :] = wf[f, 0:1, :]

    def mask():
        cells = rows * columns // LANES
        total = key_ref.shape[1]
        chunk = 512 if total % 512 == 0 else total
        cell_of = lax.broadcasted_iota(jnp.int32, (cells, chunk), 0)
        lane_of = lax.broadcasted_iota(jnp.int32, (LANES, chunk), 0)
        hits = jnp.zeros((cells, LANES), f32)
        for start in range(0, total, chunk):
            keys = key_ref[:, start:start + chunk]
            lanes = lane_ref[:, start:start + chunk]
            left = jnp.where(cell_of == keys, 1.0, 0.0).astype(bf16)
            right = jnp.where(lane_of == lanes, 1.0, 0.0).astype(bf16)
            hits = hits + lax.dot_general(
                left, right, (((1,), (1,)), ((), ())), preferred_element_type=f32
            )
        kept = jnp.where(hits > 0.5, 0.0, 1.0)
        for c in range(columns // LANES):
            keep[:, c * LANES:(c + 1) * LANES] = kept[c * rows:(c + 1) * rows]

    def field(f):
        for piece in range(PIECES):
            n = f * PIECES + piece
            span = slice(piece * part, (piece + 1) * part)
            across(n).wait_recv()
            sm[span, :] = (sums[n] + wide(yb, n)) * keep[span, :]
        total = sm[...]
        factor = share(f)
        flux = (wf[f] * tile_dot(total)).astype(bf16).astype(f32)
        acc_f[...] += factor * flux
        scaled = factor * wf[f]
        acc_s[...] += scaled * total
        acc_d[...] += scaled * slope(total, 0.0, 0.0)
        up_e[pl.ds(f, 1), :] = sm[rows - 1:rows, :]
        dn_e[pl.ds(f, 1), :] = sm[0:1, :]
        up_e[fields:fields + 1, :] += factor * wf[f, rows - 1:rows, :] * sm[rows - 2:rows - 1, :]
        dn_e[fields:fields + 1, :] += factor * wf[f, 0:1, :] * sm[1:2, :]

    @pl.loop(0, fields)
    def _(f):
        @pl.when(is_outer)
        def _():
            @pl.loop(0, PIECES)
            def _(piece):
                outer_piece(f * PIECES + piece)

        @pl.when(is_inner)
        def _():
            @pl.loop(0, PIECES)
            def _(piece):
                inner_piece(f * PIECES + piece)

        filter_sky(f)

        @pl.when(f == 0)
        def _():
            mask()

        @pl.when((f == fields - 1) & has_above)
        def _():
            wiener_up.start()

        @pl.when((f == fields - 1) & has_below)
        def _():
            wiener_down.start()

        @pl.when(f > 0)
        def _():
            field(f - 1)

    field(fields - 1)

    @pl.when(has_above)
    def _():
        edge_up.start()

    @pl.when(has_below)
    def _():
        edge_down.start()

    sm[...] = tile_dot(acc_f[...])

    @pl.when(has_above)
    def _():
        wiener_down.wait_recv()
        edge_down.wait_recv()

    @pl.when(has_below)
    def _():
        wiener_up.wait_recv()
        edge_up.wait_recv()

    zero = jnp.zeros((1, columns), f32)
    top, bottom = zero, zero
    after, before = ab_e[fields:fields + 1, :], -bl_e[fields:fields + 1, :]
    for f in range(fields):
        factor = 1.0 if f == 0 else -1.0 / (fields - 1)
        one = slice(f, f + 1)
        top = top + factor * wf[f, rows - 1:rows, :] * ab_e[one, :]
        bottom = bottom - factor * wf[f, 0:1, :] * bl_e[one, :]
        after = after - factor * ab_w[one, :] * up_e[one, :]
        before = before + factor * bl_w[one, :] * dn_e[one, :]
    flux_dec = acc_d[...] + jnp.where(row_of == rows - 1, top * 0.5, 0.0)
    flux_dec = flux_dec + jnp.where(row_of == 0, bottom * 0.5, 0.0)
    divergence = sm[...] + slope(flux_dec, before * 0.5, after * 0.5)
    out_ref[...] = -divergence - resp_ref[...] * acc_s[...]

    @pl.when(has_above)
    def _():
        wiener_up.wait_send()
        edge_up.wait_send()

    @pl.when(has_below)
    def _():
        wiener_down.wait_send()
        edge_down.wait_send()

    @pl.when(is_outer)
    def _():
        @pl.loop(0, count)
        def _(n):
            give(n).wait_send()
            across(n).wait_send()

    @pl.when(is_inner)
    def _():
        @pl.loop(0, count)
        def _(n):
            own(n).wait_send()
            relay(n).wait_send()
            to_a(n).wait_send()
            to_b(n).wait_send()
            across(n).wait_send()


def on_device(
    sky_maps,
    ivf_maps,
    sim_sky,
    sim_ivf,
    ra_wiener,
    ra_gradient,
    pair_table,
    sim_index,
    source_pixels,
    response,
):
    nsplit = pair_table.shape[0]
    axis_count = lax.axis_size("sim")
    group_bands = axis_count // nsplit
    logical = (lax.axis_index("sim") - group_bands // 2) % axis_count
    band_index = logical % group_bands
    rows, columns = sky_maps.shape
    fields = sim_index.shape[0] + 1
    sky, ivf = choose(sim_index, sky_maps, ivf_maps, sim_sky, sim_ivf)
    row = source_pixels // columns - band_index * rows
    place = source_pixels % columns
    inside = (row >= 0) & (row < rows)
    keys = jnp.where(inside, (place // LANES) * rows + row, -1)
    weight_rows = lax.dynamic_slice_in_dim(response, band_index * rows, rows)
    shape = (fields * PIECES, rows // PIECES, columns)
    slab_rows = -(-(fields + 1) // SLAB) * SLAB
    piece = pltpu.VMEM(shape, ivf.dtype)
    plane = pltpu.VMEM((rows, columns), jnp.float32)
    slabs = pltpu.VMEM((slab_rows, columns), jnp.float32)
    vmem = pl.BlockSpec(memory_space=pltpu.VMEM)
    return pl.pallas_call(
        functools.partial(estimator, nsplit),
        out_shape=jax.ShapeDtypeStruct((rows, columns), jnp.float32),
        in_specs=[pl.BlockSpec(memory_space=pltpu.SMEM)] + [vmem] * 7,
        out_specs=vmem,
        scratch_shapes=[piece] * 9
        + [pltpu.VMEM(shape, jnp.float32), plane, plane]
        + [pltpu.VMEM((fields, rows, columns), jnp.float32), plane, plane, plane]
        + [slabs] * 8
        + [pltpu.SemaphoreType.DMA((6, shape[0])), pltpu.SemaphoreType.DMA((6, shape[0]))]
        + [pltpu.SemaphoreType.DMA((4,)), pltpu.SemaphoreType.DMA((4,))],
        compiler_params=pltpu.CompilerParams(
            collective_id=0, has_side_effects=True, vmem_limit_bytes=56 << 20
        ),
    )(
        pair_table, ivf.reshape(shape), sky, ra_wiener, ra_gradient,
        keys[None], (place % LANES)[None], weight_rows[:, None],
    )


def solution(mesh):
    in_specs = (
        P(("patch", "sim"), None),
        P(("patch", "sim"), None),
        P(None, ("patch", "sim"), None),
        P(None, ("patch", "sim"), None),
        P(),
        P(),
        P(),
        P(),
        P("patch"),
        P("patch"),
    )
    out_specs = P(("patch", "sim"), None)
    return jax.shard_map(
        on_device, mesh=mesh, in_specs=in_specs, out_specs=out_specs, check_vma=False
    )
```

time: 144 us -> 96.4 us (0.67)
  the two profiles are of different devices: /device:TPU:0 before, /device:TPU:1 now
where the time goes in v2:
time: 96.4 us; the launch traced here: 96.1 us
  Pallas kernels  91.4 us (95%)
  local copies, waits for them, and re-layouts  3.31 us (3%)
  other arithmetic  1.36 us (1%)
    pallas_call x1, Pallas kernels, on_device(): pl.pallas_call(functools.partial(estimator, nsplit), out_shape=jax.ShapeD...  85.9 us
    pallas_call x1, Pallas kernels, choose(): pl.pallas_call(pick, grid_spec=pltpu.PrefetchScalarGridSpec(num_scalar_pr...  5.49 us
    unnamed x3, local copies, waits for them, and re-layouts  2.53 us

profile of v2, /device:TPU:1, one launch (start us, length us, event | category | flops | bytes accessed | tf_op | source)
XLA Modules:
  0.0 96.1 jit_solution(12576879573426257500)
XLA Ops:
  0.0 0.0 copy-start
  0.0 0.7 copy-done
  0.7 0.1 dynamic-slice_bitcast_fusion
  0.7 0.7 copy.11.resp_ref
  1.4 1.4 %add_select_fusion = (s32[4096]{0:T(1024)}, s32[4096]{0:T(1024)}) fusion(s32[4096]{0:T(1024)} %param.18, s32[]{:T(128)S(6)} %mul.7), kind=kLoop, calls=%fused_computation | loop fusion | flops 184320 | bytes 49156 | tf_op jit(solution)/shard_map/jit(remainder)/select_n | solution.py:441
  2.8 5.5 %shard_map.100 = (bf16[5,64,2048]{2,1,0:T(8,128)(2,1)}, bf16[5,64,2048]{2,1,0:T(8,128)(2,1)}) custom-call(s32[4]{0:T(128)} %index_ref.1, bf16[64,2048]{1,0:T(8,128)(2,1)} %maps_a.1, bf16[64,2048]{1,0:T(8,128)(2,1)} %maps_b.1, bf16[8,64,2048]{2,1,0:T(8,128)(2,1)} %sim_a.1, bf16[8,64,2048]{2,1,0:T(8,128)(2,1)} %sim_b.1), custom_call_target="tpu_custom_call" | custom-call | tf_op jit(solution)/shard_map/pallas_call | solution.py:35
  8.3 85.9 %shard_map.101 = f32[64,2048]{1,0:T(8,128)} custom-call(s32[8,8]{1,0:T(8,128)} %pair_ref.1, bf16[10,32,2048]{2,1,0:T(8,128)(2,1)} %bitcast.5, bf16[5,64,2048]{2,1,0:T(8,128)(2,1)} %get-tuple-element.8.sky_ref, bf16[1024,1024]{1,0:T(8,128)(2,1)} %wiener_ref.1, bf16[1024,1024]{1,0:T(8,128)(2,1)} %grad_ref.1, s32[1,4096]{1,0:T(1,128)} %bitcast.7, ...), custom_call_target="tpu_custom_call" | custom-call | tf_op jit(solution)/shard_map/pallas_call | solution.py:425
  94.2 1.9 %copy.13 = f32[64,2048]{1,0:T(8,128)} copy(f32[64,2048]{1,0:T(8,128)} %shard_map.101) | data formatting | bytes 1048576
Async XLA Ops:
  0.0 0.7 copy-start

commit v3 on v2

--- a/solution.py
+++ b/solution.py
@@ -7,45 +7,44 @@
 from jax.experimental.pallas import tpu as pltpu
 from jax.sharding import PartitionSpec as P
 
-PIECES = 2
+PIECES = 4
 LANES = 128
 SLAB = 8
 MESH = pl.DeviceIdType.MESH
 
 
-def pick(index_ref, maps_a, maps_b, sim_a, sim_b, out_a, out_b):
-    @pl.when(pl.program_id(0) == 0)
-    def _():
-        out_a[0] = maps_a[...]
-        out_b[0] = maps_b[...]
-
-    @pl.when(pl.program_id(0) > 0)
-    def _():
-        out_a[...] = sim_a[...]
-        out_b[...] = sim_b[...]
+def pick(index_ref, maps_a, maps_b, sim_a, sim_b, out_a, out_b, sems):
+    fields = out_a.shape[0]
+    copies = []
+    for f in range(fields):
+        for side, (maps, sim, out) in enumerate(((maps_b, sim_b, out_b), (maps_a, sim_a, out_a))):
+            source = maps if f == 0 else sim.at[index_ref[f - 1]]
+            copies.append(pltpu.make_async_copy(source, out.at[f], sems.at[side, f]))
+    for one in copies:
+        one.start()
+    for one in copies:
+        one.wait()
 
 
 def choose(sim_index, maps_a, maps_b, sim_a, sim_b):
     rows, columns = maps_a.shape
     fields = sim_index.shape[0] + 1
-    whole = pl.BlockSpec((rows, columns), lambda f, ids: (0, 0))
-    picked = pl.BlockSpec((1, rows, columns), lambda f, ids: (ids[jnp.maximum(f - 1, 0)], 0, 0))
-    placed = pl.BlockSpec((1, rows, columns), lambda f, ids: (f, 0, 0))
+    away = pl.BlockSpec(memory_space=pl.ANY)
+    vmem = pl.BlockSpec(memory_space=pltpu.VMEM)
     shape = jax.ShapeDtypeStruct((fields, rows, columns), maps_a.dtype)
     return pl.pallas_call(
         pick,
-        grid_spec=pltpu.PrefetchScalarGridSpec(
-            num_scalar_prefetch=1, grid=(fields,),
-            in_specs=[whole, whole, picked, picked], out_specs=[placed, placed],
-        ),
+        in_specs=[pl.BlockSpec(memory_space=pltpu.SMEM)] + [away] * 4,
+        out_specs=[vmem, vmem],
         out_shape=[shape, shape],
+        scratch_shapes=[pltpu.SemaphoreType.DMA((2, fields))],
     )(sim_index, maps_a, maps_b, sim_a, sim_b)
 
 
 def estimator(
     nsplit, pair_ref, x_ref, sky_ref, wiener_ref, grad_ref, key_ref, lane_ref, resp_ref, out_ref,
     ro, r1, r2, ra, rb, yb, pa, pb, bb, sums, keep, sm, wf, acc_f, acc_d, acc_s,
-    up_w, dn_w, bl_w, ab_w, up_e, dn_e, bl_e, ab_e, send, recv, slab_send, slab_recv,
+    up_w, dn_w, bl_w, ab_w, up_e, dn_e, bl_e, ab_e, hits, send, recv, slab_send, slab_recv,
 ):
     count = x_ref.shape[0]
     fields, rows, columns = sky_ref.shape
@@ -174,7 +173,7 @@
 
     @pl.when(is_inner)
     def _():
-        @pl.loop(0, 2)
+        @pl.loop(0, PIECES)
         def _(n):
             forward(n)
 
@@ -211,9 +210,9 @@
         sums[n] = wide(ra, n)
 
     def inner_piece(n):
-        @pl.when(n + 2 < count)
+        @pl.when(n + PIECES < count)
         def _():
-            forward(n + 2)
+            forward(n + PIECES)
 
         own(n).wait_recv()
         relay(n).wait_recv()
@@ -257,76 +256,89 @@
         up_w[pl.ds(f, 1), :] = wf[f, rows - 1:rows, :]
         dn_w[pl.ds(f, 1), :] = wf[f, 0:1, :]
 
-    def mask():
-        cells = rows * columns // LANES
-        total = key_ref.shape[1]
-        chunk = 512 if total % 512 == 0 else total
-        cell_of = lax.broadcasted_iota(jnp.int32, (cells, chunk), 0)
-        lane_of = lax.broadcasted_iota(jnp.int32, (LANES, chunk), 0)
-        hits = jnp.zeros((cells, LANES), f32)
-        for start in range(0, total, chunk):
-            keys = key_ref[:, start:start + chunk]
-            lanes = lane_ref[:, start:start + chunk]
-            left = jnp.where(cell_of == keys, 1.0, 0.0).astype(bf16)
-            right = jnp.where(lane_of == lanes, 1.0, 0.0).astype(bf16)
-            hits = hits + lax.dot_general(
-                left, right, (((1,), (1,)), ((), ())), preferred_element_type=f32
-            )
-        kept = jnp.where(hits > 0.5, 0.0, 1.0)
+    cells = rows * columns // LANES
+    sources = key_ref.shape[1] // PIECES
+
+    def mask(piece):
+        cell_of = lax.broadcasted_iota(jnp.int32, (cells, sources), 0)
+        lane_of = lax.broadcasted_iota(jnp.int32, (LANES, sources), 0)
+        span = slice(piece * sources, (piece + 1) * sources)
+        left = jnp.where(cell_of == key_ref[:, span], 1.0, 0.0).astype(bf16)
+        right = jnp.where(lane_of == lane_ref[:, span], 1.0, 0.0).astype(bf16)
+        found = lax.dot_general(left, right, (((1,), (1,)), ((), ())), preferred_element_type=f32)
+        hits[...] = found if piece == 0 else hits[...] + found
+
+    def mask_done():
         for c in range(columns // LANES):
-            keep[:, c * LANES:(c + 1) * LANES] = kept[c * rows:(c + 1) * rows]
-
-    def field(f):
+            block = hits[c * rows:(c + 1) * rows]
+            keep[:, c * LANES:(c + 1) * LANES] = jnp.where(block > 0.5, 0.0, 1.0)
+
+    def assemble(f):
         for piece in range(PIECES):
             n = f * PIECES + piece
             span = slice(piece * part, (piece + 1) * part)
             across(n).wait_recv()
             sm[span, :] = (sums[n] + wide(yb, n)) * keep[span, :]
-        total = sm[...]
         factor = share(f)
-        flux = (wf[f] * tile_dot(total)).astype(bf16).astype(f32)
-        acc_f[...] += factor * flux
-        scaled = factor * wf[f]
-        acc_s[...] += scaled * total
-        acc_d[...] += scaled * slope(total, 0.0, 0.0)
         up_e[pl.ds(f, 1), :] = sm[rows - 1:rows, :]
         dn_e[pl.ds(f, 1), :] = sm[0:1, :]
         up_e[fields:fields + 1, :] += factor * wf[f, rows - 1:rows, :] * sm[rows - 2:rows - 1, :]
         dn_e[fields:fields + 1, :] += factor * wf[f, 0:1, :] * sm[1:2, :]
 
+    def plain_terms(f):
+        total = sm[...]
+        scaled = share(f) * wf[f]
+        acc_s[...] += scaled * total
+        acc_d[...] += scaled * slope(total, 0.0, 0.0)
+
+    def tile_term(f):
+        flux = (wf[f] * tile_dot(sm[...])).astype(bf16).astype(f32)
+        acc_f[...] += share(f) * flux
+
+    def between(f, piece):
+        if piece == 0:
+            filter_sky(f)
+
+        @pl.when(f == 0)
+        def _():
+            mask(piece)
+            if piece == PIECES - 1:
+                mask_done()
+
+        if piece == 0:
+            @pl.when((f == fields - 1) & has_above)
+            def _():
+                wiener_up.start()
+
+            @pl.when((f == fields - 1) & has_below)
+            def _():
+                wiener_down.start()
+
+        @pl.when(f > 0)
+        def _():
+            if piece == 1:
+                assemble(f - 1)
+                plain_terms(f - 1)
+            if piece == 2:
+                tile_term(f - 1)
+
     @pl.loop(0, fields)
     def _(f):
-        @pl.when(is_outer)
-        def _():
-            @pl.loop(0, PIECES)
-            def _(piece):
-                outer_piece(f * PIECES + piece)
-
-        @pl.when(is_inner)
-        def _():
-            @pl.loop(0, PIECES)
-            def _(piece):
-                inner_piece(f * PIECES + piece)
-
-        filter_sky(f)
-
-        @pl.when(f == 0)
-        def _():
-            mask()
-
-        @pl.when((f == fields - 1) & has_above)
-        def _():
-            wiener_up.start()
-
-        @pl.when((f == fields - 1) & has_below)
-        def _():
-            wiener_down.start()
-
-        @pl.when(f > 0)
-        def _():
-            field(f - 1)
-
-    field(fields - 1)
+        for piece in range(PIECES):
+            n = f * PIECES + piece
+
+            @pl.when(is_outer)
+            def _():
+                outer_piece(n)
+
+            @pl.when(is_inner)
+            def _():
+                inner_piece(n)
+
+            between(f, piece)
+
+    assemble(fields - 1)
+    plain_terms(fields - 1)
 
     @pl.when(has_above)
     def _():
@@ -336,6 +348,7 @@
     def _():
         edge_down.start()
 
+    tile_term(fields - 1)
     sm[...] = tile_dot(acc_f[...])
 
     @pl.when(has_above)
@@ -431,6 +444,7 @@
         + [pltpu.VMEM(shape, jnp.float32), plane, plane]
         + [pltpu.VMEM((fields, rows, columns), jnp.float32), plane, plane, plane]
         + [slabs] * 8
+        + [pltpu.VMEM((rows * columns // LANES, LANES), jnp.float32)]
         + [pltpu.SemaphoreType.DMA((6, shape[0])), pltpu.SemaphoreType.DMA((6, shape[0]))]
         + [pltpu.SemaphoreType.DMA((4,)), pltpu.SemaphoreType.DMA((4,))],
         compiler_params=pltpu.CompilerParams(

time: 96.4 us -> 92.8 us (0.963)
  Pallas kernels: 91.4 us -> 87.8 us
    pallas_call x1, Pallas kernels: 85.9 us -> 83.9 us  [on_device(): pl.pallas_call(functools.partial(estimator, nsplit), out_shape=jax.ShapeD...]
    pallas_call x1, Pallas kernels: 5.49 us -> 3.94 us  [choose(): pl.pallas_call(pick, in_specs=[pl.BlockSpec(memory_space=pltpu.SMEM)] + [...]
where the time goes in v3:
time: 92.8 us; the launch traced here: 92.5 us
  Pallas kernels  87.8 us (95%)
  local copies, waits for them, and re-layouts  3.31 us (4%)
  other arithmetic  1.36 us (1%)
    pallas_call x1, Pallas kernels, on_device(): pl.pallas_call(functools.partial(estimator, nsplit), out_shape=jax.ShapeD...  83.9 us
    pallas_call x1, Pallas kernels, choose(): pl.pallas_call(pick, in_specs=[pl.BlockSpec(memory_space=pltpu.SMEM)] + [...  3.94 us
    unnamed x3, local copies, waits for them, and re-layouts  2.53 us

profile of v3, /device:TPU:1, one launch (start us, length us, event | category | flops | bytes accessed | tf_op | source)
XLA Modules:
  0.0 92.5 jit_solution(3936981500395004322)
XLA Ops:
  0.0 0.0 copy-start
  0.0 0.7 copy-done
  0.7 0.1 dynamic-slice_bitcast_fusion
  0.7 0.7 copy.11.resp_ref
  1.4 1.4 %add_select_fusion = (s32[4096]{0:T(1024)}, s32[4096]{0:T(1024)}) fusion(s32[4096]{0:T(1024)} %param.18, s32[]{:T(128)S(6)} %mul.7), kind=kLoop, calls=%fused_computation | loop fusion | flops 184320 | bytes 49156 | tf_op jit(solution)/shard_map/jit(remainder)/select_n | solution.py:455
  2.8 3.9 %shard_map.100 = (bf16[5,64,2048]{2,1,0:T(8,128)(2,1)}, bf16[5,64,2048]{2,1,0:T(8,128)(2,1)}) custom-call(s32[4]{0:T(128)} %index_ref.1, bf16[64,2048]{1,0:T(8,128)(2,1)} %maps_a.1, bf16[64,2048]{1,0:T(8,128)(2,1)} %maps_b.1, bf16[8,64,2048]{2,1,0:T(8,128)(2,1)} %sim_a.1, bf16[8,64,2048]{2,1,0:T(8,128)(2,1)} %sim_b.1), custom_call_target="tpu_custom_call" | custom-call | tf_op jit(solution)/shard_map/pallas_call | solution.py:35
  6.8 83.9 %shard_map.101 = f32[64,2048]{1,0:T(8,128)} custom-call(s32[8,8]{1,0:T(8,128)} %pair_ref.1, bf16[20,16,2048]{2,1,0:T(8,128)(2,1)} %bitcast.5, bf16[5,64,2048]{2,1,0:T(8,128)(2,1)} %get-tuple-element.8.sky_ref, bf16[1024,1024]{1,0:T(8,128)(2,1)} %wiener_ref.1, bf16[1024,1024]{1,0:T(8,128)(2,1)} %grad_ref.1, s32[1,4096]{1,0:T(1,128)} %bitcast.7, ...), custom_call_target="tpu_custom_call" | custom-call | tf_op jit(solution)/shard_map/pallas_call | solution.py:438
  90.6 1.9 %copy.13 = f32[64,2048]{1,0:T(8,128)} copy(f32[64,2048]{1,0:T(8,128)} %shard_map.101) | data formatting | bytes 1048576
Async XLA Ops:
  0.0 0.7 copy-start

commit v4 on v3

--- a/solution.py
+++ b/solution.py
@@ -42,7 +42,8 @@
 
 
 def estimator(
-    nsplit, pair_ref, x_ref, sky_ref, wiener_ref, grad_ref, key_ref, lane_ref, resp_ref, out_ref,
+    nsplit, pair_ref, x_ref, sky_far, wiener_far, grad_far, pixel_ref, resp_ref, out_ref,
+    sky_ref, wiener_ref, grad_ref, key_ref, lane_ref, fetch,
     ro, r1, r2, ra, rb, yb, pa, pb, bb, sums, keep, sm, wf, acc_f, acc_d, acc_s,
     up_w, dn_w, bl_w, ab_w, up_e, dn_e, bl_e, ab_e, hits, send, recv, slab_send, slab_recv,
 ):
@@ -138,6 +139,12 @@
         copy(0, n, x_ref, ro, outer).wait_recv()
         relay(n).start()
 
+    fetches = [
+        pltpu.make_async_copy(wiener_far, wiener_ref, fetch.at[0]),
+        pltpu.make_async_copy(sky_far, sky_ref, fetch.at[1]),
+        pltpu.make_async_copy(grad_far, grad_ref, fetch.at[2]),
+    ]
+
     barrier = pltpu.get_barrier_semaphore()
 
     def greet(target):
@@ -177,6 +184,16 @@
         def _(n):
             forward(n)
 
+    for one in fetches:
+        one.start()
+
+    pixel = pixel_ref[...]
+    pixel_row = (pixel >> (columns.bit_length() - 1)) - band * rows
+    pixel_column = pixel & (columns - 1)
+    block = pixel_column >> (LANES.bit_length() - 1)
+    inside = (pixel_row >= 0) & (pixel_row < rows)
+    key_ref[...] = jnp.where(inside, block * rows + pixel_row, -1)
+    lane_ref[...] = pixel_column & (LANES - 1)
     acc_f[...] = jnp.zeros_like(acc_f)
     acc_d[...] = jnp.zeros_like(acc_d)
     acc_s[...] = jnp.zeros_like(acc_s)
@@ -321,6 +338,9 @@
                 plain_terms(f - 1)
             if piece == 2:
                 tile_term(f - 1)
+
+    for one in fetches:
+        one.wait()
 
     @pl.loop(0, fields)
     def _(f):
@@ -374,7 +394,11 @@
     flux_dec = acc_d[...] + jnp.where(row_of == rows - 1, top * 0.5, 0.0)
     flux_dec = flux_dec + jnp.where(row_of == 0, bottom * 0.5, 0.0)
     divergence = sm[...] + slope(flux_dec, before * 0.5, after * 0.5)
-    out_ref[...] = -divergence - resp_ref[...] * acc_s[...]
+    span = resp_ref.shape[1]
+    row_at = lax.broadcasted_iota(jnp.int32, (rows, span), 0) + band * rows
+    lane_at = lax.broadcasted_iota(jnp.int32, (rows, span), 1)
+    ratios = jnp.sum(jnp.where(row_at == lane_at, resp_ref[...], 0.0), axis=1, keepdims=True)
+    out_ref[...] = -divergence - ratios * acc_s[...]
 
     @pl.when(has_above)
     def _():
@@ -417,30 +441,26 @@
     response,
 ):
     nsplit = pair_table.shape[0]
-    axis_count = lax.axis_size("sim")
-    group_bands = axis_count // nsplit
-    logical = (lax.axis_index("sim") - group_bands // 2) % axis_count
-    band_index = logical % group_bands
     rows, columns = sky_maps.shape
     fields = sim_index.shape[0] + 1
+    assert columns & (columns - 1) == 0
     sky, ivf = choose(sim_index, sky_maps, ivf_maps, sim_sky, sim_ivf)
-    row = source_pixels // columns - band_index * rows
-    place = source_pixels % columns
-    inside = (row >= 0) & (row < rows)
-    keys = jnp.where(inside, (place // LANES) * rows + row, -1)
-    weight_rows = lax.dynamic_slice_in_dim(response, band_index * rows, rows)
     shape = (fields * PIECES, rows // PIECES, columns)
     slab_rows = -(-(fields + 1) // SLAB) * SLAB
     piece = pltpu.VMEM(shape, ivf.dtype)
     plane = pltpu.VMEM((rows, columns), jnp.float32)
     slabs = pltpu.VMEM((slab_rows, columns), jnp.float32)
     vmem = pl.BlockSpec(memory_space=pltpu.VMEM)
+    away = pl.BlockSpec(memory_space=pl.ANY)
+    pixels = pltpu.VMEM((1, source_pixels.shape[0]), jnp.int32)
+    matrix = pltpu.VMEM(ra_wiener.shape, ra_wiener.dtype)
     return pl.pallas_call(
         functools.partial(estimator, nsplit),
         out_shape=jax.ShapeDtypeStruct((rows, columns), jnp.float32),
-        in_specs=[pl.BlockSpec(memory_space=pltpu.SMEM)] + [vmem] * 7,
+        in_specs=[pl.BlockSpec(memory_space=pltpu.SMEM), vmem] + [away] * 3 + [vmem] * 2,
         out_specs=vmem,
-        scratch_shapes=[piece] * 9
+        scratch_shapes=[pltpu.VMEM(sky.shape, sky.dtype), matrix, matrix, pixels, pixels]
+        + [pltpu.SemaphoreType.DMA((3,))] + [piece] * 9
         + [pltpu.VMEM(shape, jnp.float32), plane, plane]
         + [pltpu.VMEM((fields, rows, columns), jnp.float32), plane, plane, plane]
         + [slabs] * 8
@@ -452,7 +472,7 @@
         ),
     )(
         pair_table, ivf.reshape(shape), sky, ra_wiener, ra_gradient,
-        keys[None], (place % LANES)[None], weight_rows[:, None],
+        source_pixels[None], response[None],
     )
 
 

time: 92.8 us -> 88.5 us (0.954)
  local copies, waits for them, and re-layouts: 3.31 us -> 1.87 us
  Pallas kernels: 87.8 us -> 86.4 us
  other arithmetic: 1.36 us -> 0 us
    pallas_call x1, Pallas kernels: 83.9 us -> 82.5 us  [on_device(): pl.pallas_call(functools.partial(estimator, nsplit), out_shape=jax.ShapeD...]
    select_n x1 -> x0, other arithmetic: 1.36 us -> none  [on_device(): place % LANES]
    unnamed x3 -> x1, local copies, waits for them, and re-layouts: 2.53 us -> 1.87 us
where the time goes in v4:
time: 88.5 us; the launch traced here: 88.3 us
  Pallas kernels  86.4 us (98%)
  local copies, waits for them, and re-layouts  1.87 us (2%)
    pallas_call x1, Pallas kernels, on_device(): pl.pallas_call(functools.partial(estimator, nsplit), out_shape=jax.ShapeD...  82.5 us
    pallas_call x1, Pallas kernels, choose(): pl.pallas_call(pick, in_specs=[pl.BlockSpec(memory_space=pltpu.SMEM)] + [...  3.93 us
    unnamed x1, local copies, waits for them, and re-layouts  1.87 us

profile of v4, /device:TPU:1, one launch (start us, length us, event | category | flops | bytes accessed | tf_op | source)
XLA Modules:
  0.0 88.3 jit_solution(11648946456380123438)
XLA Ops:
  0.0 3.9 %shard_map.100 = (bf16[5,64,2048]{2,1,0:T(8,128)(2,1)}, bf16[5,64,2048]{2,1,0:T(8,128)(2,1)}) custom-call(s32[4]{0:T(128)} %index_ref.1, bf16[64,2048]{1,0:T(8,128)(2,1)} %maps_a.1, bf16[64,2048]{1,0:T(8,128)(2,1)} %maps_b.1, bf16[8,64,2048]{2,1,0:T(8,128)(2,1)} %sim_a.1, bf16[8,64,2048]{2,1,0:T(8,128)(2,1)} %sim_b.1), custom_call_target="tpu_custom_call" | custom-call | tf_op jit(solution)/shard_map/pallas_call | solution.py:35
  3.9 82.5 %shard_map.101 = f32[64,2048]{1,0:T(8,128)} custom-call(s32[8,8]{1,0:T(8,128)} %pair_ref.1, bf16[20,16,2048]{2,1,0:T(8,128)(2,1)} %bitcast.3, bf16[5,64,2048]{2,1,0:T(8,128)(2,1)} %get-tuple-element.8.sky_far, bf16[1024,1024]{1,0:T(8,128)(2,1)} %wiener_far.1, bf16[1024,1024]{1,0:T(8,128)(2,1)} %grad_far.1, s32[1,4096]{1,0:T(1,128)} %bitcast.4, f32[1,128]{1,0:T(1,128)} %bitcast.5), custom_call_target="tpu_custom_call" | custom-call | tf_op jit(solution)/shard_map/pallas_call | solution.py:457
  86.4 1.9 %copy.12 = f32[64,2048]{1,0:T(8,128)} copy(f32[64,2048]{1,0:T(8,128)} %shard_map.101) | data formatting | bytes 1048576

commit v5 on v4

--- a/solution.py
+++ b/solution.py
@@ -13,42 +13,38 @@
 MESH = pl.DeviceIdType.MESH
 
 
-def pick(index_ref, maps_a, maps_b, sim_a, sim_b, out_a, out_b, sems):
-    fields = out_a.shape[0]
+def pick(index_ref, maps, sim, out, sems):
     copies = []
-    for f in range(fields):
-        for side, (maps, sim, out) in enumerate(((maps_b, sim_b, out_b), (maps_a, sim_a, out_a))):
-            source = maps if f == 0 else sim.at[index_ref[f - 1]]
-            copies.append(pltpu.make_async_copy(source, out.at[f], sems.at[side, f]))
+    for f in range(out.shape[0]):
+        source = maps if f == 0 else sim.at[index_ref[f - 1]]
+        copies.append(pltpu.make_async_copy(source, out.at[f], sems.at[f]))
     for one in copies:
         one.start()
     for one in copies:
         one.wait()
 
 
-def choose(sim_index, maps_a, maps_b, sim_a, sim_b):
-    rows, columns = maps_a.shape
+def choose(sim_index, maps, sim):
     fields = sim_index.shape[0] + 1
     away = pl.BlockSpec(memory_space=pl.ANY)
-    vmem = pl.BlockSpec(memory_space=pltpu.VMEM)
-    shape = jax.ShapeDtypeStruct((fields, rows, columns), maps_a.dtype)
     return pl.pallas_call(
         pick,
-        in_specs=[pl.BlockSpec(memory_space=pltpu.SMEM)] + [away] * 4,
-        out_specs=[vmem, vmem],
-        out_shape=[shape, shape],
-        scratch_shapes=[pltpu.SemaphoreType.DMA((2, fields))],
-    )(sim_index, maps_a, maps_b, sim_a, sim_b)
+        in_specs=[pl.BlockSpec(memory_space=pltpu.SMEM), away, away],
+        out_specs=pl.BlockSpec(memory_space=pltpu.VMEM),
+        out_shape=jax.ShapeDtypeStruct((fields,) + maps.shape, maps.dtype),
+        scratch_shapes=[pltpu.SemaphoreType.DMA((fields,))],
+    )(sim_index, maps, sim)
 
 
 def estimator(
-    nsplit, pair_ref, x_ref, sky_far, wiener_far, grad_far, pixel_ref, resp_ref, out_ref,
+    nsplit, pair_ref, index_ref, x_ref, maps_far, sim_far, wiener_far, grad_far, pixel_ref, resp_ref, out_ref,
     sky_ref, wiener_ref, grad_ref, key_ref, lane_ref, fetch,
     ro, r1, r2, ra, rb, yb, pa, pb, bb, sums, keep, sm, wf, acc_f, acc_d, acc_s,
     up_w, dn_w, bl_w, ab_w, up_e, dn_e, bl_e, ab_e, hits, send, recv, slab_send, slab_recv,
 ):
     count = x_ref.shape[0]
-    fields, rows, columns = sky_ref.shape
+    fields = index_ref.shape[0] + 1
+    rows, columns = maps_far.shape
     part = rows // PIECES
     width = grad_ref.shape[0]
     tiles = columns // width
@@ -141,7 +137,8 @@
 
     fetches = [
         pltpu.make_async_copy(wiener_far, wiener_ref, fetch.at[0]),
-        pltpu.make_async_copy(sky_far, sky_ref, fetch.at[1]),
+        pltpu.make_async_copy(maps_far, sky_ref.at[0], fetch.at[1]),
+        pltpu.make_async_copy(sim_far, sky_ref.at[pl.ds(1, sim_far.shape[0])], fetch.at[3]),
         pltpu.make_async_copy(grad_far, grad_ref, fetch.at[2]),
     ]
 
@@ -264,7 +261,8 @@
         return jnp.where(f == 0, jnp.float32(1.0), jnp.float32(-1.0 / (fields - 1)))
 
     def filter_sky(f):
-        sky = sky_ref[f]
+        cached = index_ref[jnp.maximum(f - 1, 0)] + 1
+        sky = sky_ref[jnp.where(f == 0, 0, cached)]
         lefts = [sky[:, t * width:(t + 1) * width] for t in range(tiles)]
         result = jnp.dot(jnp.concatenate(lefts, axis=0), wiener_ref[...], preferred_element_type=f32)
         result = result.astype(bf16).astype(f32)
@@ -444,7 +442,7 @@
     rows, columns = sky_maps.shape
     fields = sim_index.shape[0] + 1
     assert columns & (columns - 1) == 0
-    sky, ivf = choose(sim_index, sky_maps, ivf_maps, sim_sky, sim_ivf)
+    ivf = choose(sim_index, ivf_maps, sim_ivf)
     shape = (fields * PIECES, rows // PIECES, columns)
     slab_rows = -(-(fields + 1) // SLAB) * SLAB
     piece = pltpu.VMEM(shape, ivf.dtype)
@@ -457,10 +455,10 @@
     return pl.pallas_call(
         functools.partial(estimator, nsplit),
         out_shape=jax.ShapeDtypeStruct((rows, columns), jnp.float32),
-        in_specs=[pl.BlockSpec(memory_space=pltpu.SMEM), vmem] + [away] * 3 + [vmem] * 2,
+        in_specs=[pl.BlockSpec(memory_space=pltpu.SMEM)] * 2 + [vmem] + [away] * 4 + [vmem] * 2,
         out_specs=vmem,
-        scratch_shapes=[pltpu.VMEM(sky.shape, sky.dtype), matrix, matrix, pixels, pixels]
-        + [pltpu.SemaphoreType.DMA((3,))] + [piece] * 9
+        scratch_shapes=[pltpu.VMEM((sim_sky.shape[0] + 1, rows, columns), sky_maps.dtype), matrix, matrix, pixels, pixels]
+        + [pltpu.SemaphoreType.DMA((4,))] + [piece] * 9
         + [pltpu.VMEM(shape, jnp.float32), plane, plane]
         + [pltpu.VMEM((fields, rows, columns), jnp.float32), plane, plane, plane]
         + [slabs] * 8
@@ -471,7 +469,7 @@
             collective_id=0, has_side_effects=True, vmem_limit_bytes=56 << 20
         ),
     )(
-        pair_table, ivf.reshape(shape), sky, ra_wiener, ra_gradient,
+        pair_table, sim_index, ivf.reshape(shape), sky_maps, sim_sky, ra_wiener, ra_gradient,
         source_pixels[None], response[None],
     )
 

time: 88.5 us -> 88 us (level)
    pallas_call x1, Pallas kernels: 3.93 us -> 3.03 us  [choose(): pl.pallas_call(pick, in_specs=[pl.BlockSpec(memory_space=pltpu.SMEM), awa...]
where the time goes in v5:
time: 88 us; the launch traced here: 87.8 us
  Pallas kernels  85.9 us (98%)
  local copies, waits for them, and re-layouts  1.87 us (2%)
    pallas_call x1, Pallas kernels, on_device(): pl.pallas_call(functools.partial(estimator, nsplit), out_shape=jax.ShapeD...  82.8 us
    pallas_call x1, Pallas kernels, choose(): pl.pallas_call(pick, in_specs=[pl.BlockSpec(memory_space=pltpu.SMEM), awa...  3.03 us
    unnamed x1, local copies, waits for them, and re-layouts  1.87 us

profile of v5, /device:TPU:1, one launch (start us, length us, event | category | flops | bytes accessed | tf_op | source)
XLA Modules:
  0.0 87.8 jit_solution(4399910677766744713)
XLA Ops:
  0.0 3.0 %shard_map.100 = bf16[5,64,2048]{2,1,0:T(8,128)(2,1)} custom-call(s32[4]{0:T(128)} %index_ref.3, bf16[64,2048]{1,0:T(8,128)(2,1)} %maps.1, bf16[8,64,2048]{2,1,0:T(8,128)(2,1)} %sim.1), custom_call_target="tpu_custom_call" | custom-call | tf_op jit(solution)/shard_map/pallas_call | solution.py:30
  3.0 82.8 %shard_map.101 = f32[64,2048]{1,0:T(8,128)} custom-call(s32[8,8]{1,0:T(8,128)} %pair_ref.1, s32[4]{0:T(128)} %index_ref.3, bf16[20,16,2048]{2,1,0:T(8,128)(2,1)} %bitcast.3, bf16[64,2048]{1,0:T(8,128)(2,1)} %maps_far.1, bf16[8,64,2048]{2,1,0:T(8,128)(2,1)} %sim_far.1, bf16[1024,1024]{1,0:T(8,128)(2,1)} %wiener_far.1, bf16[1024,1024]{1,0:T(8,128)(2,1)} %grad_far.1, ...), custom_call_target="tpu_custom_call" | custom-call | tf_op jit(solution)/shard_map/pallas_call | solution.py:455
  85.9 1.9 %copy.12 = f32[64,2048]{1,0:T(8,128)} copy(f32[64,2048]{1,0:T(8,128)} %shard_map.101) | data formatting | bytes 1048576
